TPU v7x, 128 devices: a whole 4x4x4 slice. The times are simulated.
128 devices in a mesh: shard: 2 (over y_lo), context: 16 (over x, y_hi, core), tensor: 4 (over z).
Axes of the slice: x: 4, y: 4 (y_hi: 2, y_lo: 2; y = y_hi * 2 + y_lo), z: 4, core: 2. Of those that a mesh axis runs over, the one named last changes fastest.
Arguments:
- layer_input_residual: float32 [2, 6144, 768], P('shard', 'context'), may hold values from -6 to 6
- positions: int32 [2, 6144], P('shard'), may hold values from 0 to 6143, as said below
- ln1_gain: bfloat16 [768], P(('shard', 'context')), may hold values from 0.5 to 1.5
- ln1_bias: bfloat16 [768], P(('shard', 'context')), may hold values from -3 to 3
- ln2_gain: bfloat16 [768], P(('shard', 'context')), may hold values from 0.3984375 to 2.5
- ln2_bias: bfloat16 [768], P(('shard', 'context')), may hold values from -3 to 3
- w_qkv: bfloat16 [768, 3, 768], P(('shard', 'context'), None, 'tensor'), may hold values from -0.21875 to 0.21875
- query_key_value_bias: float32 [3, 768], P(None, 'tensor'), may hold values from -9 to 9
- w_out: bfloat16 [768, 768], P(('shard', 'context'), 'tensor'), may hold values from -0.4375 to 0.4375
- b_out: bfloat16 [768], P(('shard', 'context')), may hold values from -3 to 3
- w_up: bfloat16 [768, 3072], P(('shard', 'context'), 'tensor'), may hold values from -0.21875 to 0.21875
- up_bias_vector: float32 [3072], P('tensor'), may hold values from -3 to 3
- w_down: bfloat16 [768, 3072], P(('shard', 'context'), 'tensor'), may hold values from -0.109375 to 0.109375
- b_down: bfloat16 [768], P(('shard', 'context')), may hold values from -3 to 3
- grad_out: float32 [2, 6144, 768], P('shard', 'context'), may hold values from -6 to 6
Outputs:
- layer_out: float32 [2, 6144, 768], P('shard', 'context')
- grad_in: float32 [2, 6144, 768], P('shard', 'context')
- g_ln1_gain: float32 [768], P(('shard', 'context'))
- g_ln1_bias: float32 [768], P(('shard', 'context'))
- g_ln2_gain: float32 [768], P(('shard', 'context'))
- g_ln2_bias: float32 [768], P(('shard', 'context'))
- query_key_value_weight_gradient: float32 [768, 3, 768], P(('shard', 'context'), None, 'tensor')
- g_b_qkv: float32 [3, 768], P(None, 'tensor')
- out_weight_gradient: float32 [768, 768], P(('shard', 'context'), 'tensor')
- g_b_out: float32 [768], P(('shard', 'context'))
- up_weight_gradient: float32 [768, 3072], P(('shard', 'context'), 'tensor')
- g_b_up: float32 [3072], P('tensor')
- down_weight_gradient: float32 [768, 3072], P(('shard', 'context'), 'tensor')
- g_b_down: float32 [768], P(('shard', 'context'))
Inputs may be any that keep to these rules, and one draw needn't show every extreme that they name: Each row of positions is a permutation of the positions of one sequence, made of runs of 192 consecutive positions, each run starting at a multiple of 192.
All inputs are finite; a program needn't handle non-finite values.
Results may differ from a plain program's by a relative error of at most 0.029.
The roundings to bfloat16 on the way count: a program that leaves them out, or rounds other values in their place, can miss the bound.
Values may be sent and summed in bfloat16 or wider, within the bound.
A program may use at most 128 MiB of HBM per device.

v0:
```python
import math

import jax
import jax.numpy as jnp
from jax import lax
from jax.sharding import PartitionSpec as P

HS = 64
ROT = 16


norm_eps = 1e-05


def layer_norm_forward(values):
    centered = values - jnp.mean(values, axis=-1, keepdims=True)
    inverse_deviation = lax.rsqrt(jnp.mean(centered * centered, axis=-1, keepdims=True) + norm_eps)
    return (centered * inverse_deviation, inverse_deviation)


def rotary_tables(pos_rows):
    half_rot = ROT // 2
    freqs = jnp.exp(-(jnp.arange(half_rot).astype(jnp.float32) * (2.0 / ROT)) * math.log(10000.0))
    angles = pos_rows.astype(jnp.float32)[..., None] * freqs
    return (jnp.cos(angles), jnp.sin(angles))


def rotate_heads(tensor, cosine, sine, sign_dir):
    half_rot = ROT // 2
    first = tensor[..., :half_rot]
    second = tensor[..., half_rot:ROT]
    cos_b = cosine[..., None, :]
    sin_b = sine[..., None, :] * sign_dir
    return jnp.concatenate(
        [first * cos_b - second * sin_b, second * cos_b + first * sin_b, tensor[..., ROT:]], axis=-1
    )


def gelu_slope(pre_act):
    cdf_val = 0.5 * (1.0 + jax.scipy.special.erf(pre_act * 0.7071067811865476))
    pdf_val = jnp.exp(-0.5 * pre_act * pre_act) * 0.3989422804014327
    return cdf_val + pre_act * pdf_val


def layer_norm_backward(
    norm_output_gradient, centered_scaled_input, inverse_deviation, gain_vector_rows
):
    incoming_gradient = norm_output_gradient * gain_vector_rows
    input_gradient_piece = inverse_deviation * (
        incoming_gradient
        - jnp.mean(incoming_gradient, axis=-1, keepdims=True)
        - centered_scaled_input
        * jnp.mean(incoming_gradient * centered_scaled_input, axis=-1, keepdims=True)
    )
    return (
        input_gradient_piece,
        jnp.sum(norm_output_gradient * centered_scaled_input, axis=(0, 1)),
        jnp.sum(norm_output_gradient, axis=(0, 1)),
    )


def shards(
    layer_input_residual,
    positions,
    ln1_gain,
    ln1_bias,
    ln2_gain,
    ln2_bias,
    w_qkv,
    query_key_value_bias,
    w_out,
    b_out,
    w_up,
    up_bias_vector,
    w_down,
    b_down,
    grad_out,
):
    scale = HS ** (-0.5)
    seqs_here, local_len, width = layer_input_residual.shape
    inner_here = w_qkv.shape[2]
    heads_here = inner_here // HS
    head_shape = (seqs_here, local_len, heads_here, HS)
    vec_local = jnp.stack([ln1_gain, ln1_bias, ln2_gain, ln2_bias, b_out, b_down], axis=1)
    query_key_value_whole, output_weight_whole, up_weight_whole, down_weight_whole, vec_full = (
        lax.all_gather(w_qkv, ("shard", "context"), axis=0, tiled=True),
        lax.all_gather(w_out, ("shard", "context"), axis=0, tiled=True),
        lax.all_gather(w_up, ("shard", "context"), axis=0, tiled=True),
        lax.all_gather(w_down, ("shard", "context"), axis=0, tiled=True),
        lax.all_gather(vec_local, ("shard", "context"), axis=0, tiled=True),
    )
    vec_f32 = vec_full.astype(jnp.float32)
    first_norm_gain, first_norm_bias, second_norm_gain, second_norm_bias = (
        vec_f32[:, 0],
        vec_f32[:, 1],
        vec_f32[:, 2],
        vec_f32[:, 3],
    )
    bias_sum = vec_f32[:, 4] + vec_f32[:, 5]
    ctx_index = lax.axis_index("context")
    query_pos = lax.dynamic_slice_in_dim(positions, ctx_index * local_len, local_len, 1)
    centered_scaled_input, inverse_deviation = layer_norm_forward(layer_input_residual)
    first_norm_output = (centered_scaled_input * first_norm_gain + first_norm_bias).astype(
        jnp.bfloat16
    )
    second_norm_output = (centered_scaled_input * second_norm_gain + second_norm_bias).astype(
        jnp.bfloat16
    )
    attention_projected = (
        jnp.einsum(
            "uoy,ypj->uopj",
            first_norm_output,
            query_key_value_whole,
            preferred_element_type=jnp.float32,
        )
        + query_key_value_bias
    )
    cosine, sine = rotary_tables(query_pos)
    query = rotate_heads(
        attention_projected[:, :, 0].reshape(head_shape), cosine, sine, 1.0
    ).astype(jnp.bfloat16)
    keys = rotate_heads(attention_projected[:, :, 1].reshape(head_shape), cosine, sine, 1.0).astype(
        jnp.bfloat16
    )
    keys_flat = keys.reshape(seqs_here, local_len, inner_here)
    values_flat = attention_projected[:, :, 2].astype(jnp.bfloat16)
    init_state = (
        jnp.full((seqs_here, heads_here, local_len), -1e30, jnp.float32),
        jnp.zeros((seqs_here, heads_here, local_len), jnp.float32),
        jnp.zeros((seqs_here, heads_here, local_len, HS), jnp.float32),
    )
    key_piece = lax.all_gather(keys_flat, "context", axis=1, tiled=True)
    val_piece = lax.all_gather(values_flat, "context", axis=1, tiled=True)
    count = key_piece.shape[1]
    width_blk = 512

    def inner_block(block_idx, state):
        running_max, running_sum, weighted = state
        offset = block_idx * width_blk
        key_block = lax.dynamic_slice_in_dim(key_piece, offset, width_blk, 1).reshape(
            seqs_here, width_blk, heads_here, HS
        )
        val_block = lax.dynamic_slice_in_dim(val_piece, offset, width_blk, 1).reshape(
            seqs_here, width_blk, heads_here, HS
        )
        key_pos = lax.dynamic_slice_in_dim(positions, offset, width_blk, 1)
        scores = (
            jnp.einsum("sqhd,skhd->shqk", query, key_block, preferred_element_type=jnp.float32)
            * scale
        )
        allowed = key_pos[:, None, None, :] <= query_pos[:, None, :, None]
        new_max = jnp.maximum(running_max, jnp.max(jnp.where(allowed, scores, -1e30), axis=-1))
        attn_weights = jnp.where(allowed, jnp.exp(scores - new_max[..., None]), 0.0)
        factor = jnp.exp(running_max - new_max)
        running_sum = running_sum * factor + jnp.sum(attn_weights, axis=-1)
        weighted = weighted * factor[..., None] + jnp.einsum(
            "shqk,skhd->shqd",
            attn_weights,
            val_block.astype(jnp.float32),
            precision=lax.Precision.HIGHEST,
        )
        return (new_max, running_sum, weighted)

    running_max, running_sum, weighted = lax.fori_loop(
        0, count // width_blk, inner_block, init_state
    )
    log_norm = running_max + jnp.log(running_sum)
    attended = (weighted / running_sum[..., None]).transpose(0, 2, 1, 3).astype(jnp.bfloat16)
    attention_rows_flat = attended.reshape(seqs_here, local_len, inner_here)
    pre_act = (
        jnp.einsum(
            "ceg,gp->cep", second_norm_output, up_weight_whole, preferred_element_type=jnp.float32
        )
        + up_bias_vector
    )
    gelu_output = jax.nn.gelu(pre_act, approximate=False).astype(jnp.bfloat16)
    branch_part = jnp.einsum(
        "xyn,gn->xyg", attention_rows_flat, output_weight_whole, preferred_element_type=jnp.float32
    ) + jnp.einsum(
        "ybj,oj->ybo", gelu_output, down_weight_whole, preferred_element_type=jnp.float32
    )
    summed = lax.psum(branch_part.astype(jnp.bfloat16), "tensor").astype(jnp.float32)
    layer_out = layer_input_residual + summed + bias_sum
    gradient_half_precision = grad_out.astype(jnp.bfloat16)
    g_vec_out = jnp.sum(grad_out, axis=(0, 1))
    down_weight_gradient = jnp.einsum(
        "mpc,mpv->cv", gradient_half_precision, gelu_output, preferred_element_type=jnp.float32
    )
    gelu_gradient = jnp.einsum(
        "ceg,gp->cep",
        gradient_half_precision,
        down_weight_whole,
        preferred_element_type=jnp.float32,
    )
    g_pre = gelu_gradient * gelu_slope(pre_act)
    g_b_up_part = jnp.sum(g_pre, axis=(0, 1))
    preact_gradient_half = g_pre.astype(jnp.bfloat16)
    up_weight_gradient = jnp.einsum(
        "mpc,mpv->cv", second_norm_output, preact_gradient_half, preferred_element_type=jnp.float32
    )
    norm2_output_gradient = jnp.einsum(
        "ybj,oj->ybo", preact_gradient_half, up_weight_whole, preferred_element_type=jnp.float32
    )
    out_weight_gradient = jnp.einsum(
        "bck,bcm->km",
        gradient_half_precision,
        attention_rows_flat,
        preferred_element_type=jnp.float32,
    )
    g_attended = (
        jnp.einsum(
            "yrh,hx->yrx",
            gradient_half_precision,
            output_weight_whole,
            preferred_element_type=jnp.float32,
        )
        .astype(jnp.bfloat16)
        .reshape(head_shape)
    )
    row_delta = jnp.sum(
        g_attended.astype(jnp.float32) * attended.astype(jnp.float32), axis=-1
    ).transpose(0, 2, 1)
    key_back, val_back = (
        lax.all_gather(keys_flat, "context", axis=1, tiled=True),
        lax.all_gather(values_flat, "context", axis=1, tiled=True),
    )
    full_len = key_back.shape[1]
    back_blk = 512
    zero_query = jnp.zeros((seqs_here, heads_here, local_len, HS), jnp.float32)

    def back_block(block_idx, state):
        grad_query, grad_key, grad_val = state
        offset = block_idx * back_blk
        key_block = lax.dynamic_slice_in_dim(key_back, offset, back_blk, 1).reshape(
            seqs_here, back_blk, heads_here, HS
        )
        val_block = lax.dynamic_slice_in_dim(val_back, offset, back_blk, 1).reshape(
            seqs_here, back_blk, heads_here, HS
        )
        key_pos = lax.dynamic_slice_in_dim(positions, offset, back_blk, 1)
        scores = (
            jnp.einsum("sqhd,skhd->shqk", query, key_block, preferred_element_type=jnp.float32)
            * scale
        )
        allowed = key_pos[:, None, None, :] <= query_pos[:, None, :, None]
        attn_weights = jnp.where(allowed, jnp.exp(scores - log_norm[..., None]), 0.0)
        grad_val_blk = jnp.einsum(
            "shqk,sqhd->skhd",
            attn_weights.astype(jnp.bfloat16),
            g_attended,
            preferred_element_type=jnp.float32,
        )
        g_prob = jnp.einsum(
            "sqhd,skhd->shqk", g_attended, val_block, preferred_element_type=jnp.float32
        )
        g_scores = (attn_weights * (g_prob - row_delta[..., None]) * scale).astype(jnp.bfloat16)
        grad_query = grad_query + jnp.einsum(
            "shqk,skhd->shqd", g_scores, key_block, preferred_element_type=jnp.float32
        )
        grad_key_blk = jnp.einsum(
            "shqk,sqhd->skhd", g_scores, query, preferred_element_type=jnp.float32
        )
        grad_key = lax.dynamic_update_slice_in_dim(grad_key, grad_key_blk, offset, 1)
        grad_val = lax.dynamic_update_slice_in_dim(grad_val, grad_val_blk, offset, 1)
        return (grad_query, grad_key, grad_val)

    zero_keyval = jnp.zeros((seqs_here, full_len, heads_here, HS), jnp.float32)
    grad_query, grad_key, grad_val = lax.fori_loop(
        0, full_len // back_blk, back_block, (zero_query, zero_keyval, zero_keyval)
    )
    own_key, own_val = (
        lax.psum_scatter(
            grad_key.reshape(seqs_here, full_len, inner_here),
            "context",
            scatter_dimension=1,
            tiled=True,
        ),
        lax.psum_scatter(
            grad_val.reshape(seqs_here, full_len, inner_here),
            "context",
            scatter_dimension=1,
            tiled=True,
        ),
    )
    g_query = rotate_heads(grad_query.transpose(0, 2, 1, 3), cosine, sine, -1.0)
    g_keys = rotate_heads(own_key.reshape(head_shape), cosine, sine, -1.0)
    g_projected = jnp.stack(
        [
            g_query.reshape(seqs_here, local_len, inner_here),
            g_keys.reshape(seqs_here, local_len, inner_here),
            own_val,
        ],
        axis=2,
    )
    g_b_qkv_part = jnp.sum(g_projected, axis=(0, 1))
    projection_gradient_half = g_projected.astype(jnp.bfloat16)
    query_key_value_weight_gradient = jnp.einsum(
        "znf,znwe->fwe",
        first_norm_output,
        projection_gradient_half,
        preferred_element_type=jnp.float32,
    )
    norm1_output_gradient = jnp.einsum(
        "awmn,omn->awo",
        projection_gradient_half,
        query_key_value_whole,
        preferred_element_type=jnp.float32,
    )
    norm1_output_gradient, norm2_output_gradient = lax.psum(
        (norm1_output_gradient, norm2_output_gradient), "tensor"
    )
    input_gradient_first, first_gain_gradient, first_bias_gradient = layer_norm_backward(
        norm1_output_gradient, centered_scaled_input, inverse_deviation, first_norm_gain
    )
    input_gradient_second, second_gain_gradient, second_bias_gradient = layer_norm_backward(
        norm2_output_gradient, centered_scaled_input, inverse_deviation, second_norm_gain
    )
    grad_in = grad_out + (input_gradient_first + input_gradient_second)
    norm_sums = jnp.stack(
        [first_gain_gradient, first_bias_gradient, second_gain_gradient, second_bias_gradient],
        axis=1,
    )
    vec_grads = jnp.concatenate([norm_sums, jnp.stack([g_vec_out, g_vec_out], axis=1)], axis=1)
    own_qkv, own_out, own_up, own_down, own_vec = (
        lax.psum_scatter(
            query_key_value_weight_gradient, ("shard", "context"), scatter_dimension=0, tiled=True
        ),
        lax.psum_scatter(
            out_weight_gradient, ("shard", "context"), scatter_dimension=0, tiled=True
        ),
        lax.psum_scatter(up_weight_gradient, ("shard", "context"), scatter_dimension=0, tiled=True),
        lax.psum_scatter(
            down_weight_gradient, ("shard", "context"), scatter_dimension=0, tiled=True
        ),
        lax.psum_scatter(vec_grads, ("shard", "context"), scatter_dimension=0, tiled=True),
    )
    g_b_qkv, g_b_up = lax.psum((g_b_qkv_part, g_b_up_part), ("shard", "context"))
    return (
        layer_out,
        grad_in,
        own_vec[:, 0],
        own_vec[:, 1],
        own_vec[:, 2],
        own_vec[:, 3],
        own_qkv,
        g_b_qkv,
        own_out,
        own_vec[:, 4],
        own_up,
        g_b_up,
        own_down,
        own_vec[:, 5],
    )


def solution(mesh):
    in_specs = (
        P("shard", "context", None),
        P("shard", None),
        P(("shard", "context")),
        P(("shard", "context")),
        P(("shard", "context")),
        P(("shard", "context")),
        P(("shard", "context"), None, "tensor"),
        P(None, "tensor"),
        P(("shard", "context"), "tensor"),
        P(("shard", "context")),
        P(("shard", "context"), "tensor"),
        P("tensor"),
        P(("shard", "context"), "tensor"),
        P(("shard", "context")),
        P("shard", "context", None),
    )
    out_specs = (
        P("shard", "context", None),
        P("shard", "context", None),
        P(("shard", "context")),
        P(("shard", "context")),
        P(("shard", "context")),
        P(("shard", "context")),
        P(("shard", "context"), None, "tensor"),
        P(None, "tensor"),
        P(("shard", "context"), "tensor"),
        P(("shard", "context")),
        P(("shard", "context"), "tensor"),
        P("tensor"),
        P(("shard", "context"), "tensor"),
        P(("shard", "context")),
    )
    return jax.shard_map(shards, mesh=mesh, in_specs=in_specs, out_specs=out_specs, check_vma=False)
```

profile of v0, /device:TPU:1, one launch (start us, length us, event | category | flops | bytes accessed | tf_op | source)
XLA Modules:
  0.0 1258.8 jit_solution(13562407661413741384)
XLA Ops:
  9.2 41.9 %all-gather.1 = bf16[32,24,6]{1,2,0:T(8,128)(2,1)S(1)} all-gather(bf16[1,24,6]{1,2,0:T(8,128)(2,1)S(1)} %bitcast.286), channel_id=1, replica_groups=mesh['shard'=2,'context'=16,'tensor'=4] {'shard','context'}, dimensions={0}, use_global_device_ids=true | all-gather | bytes 9504 | tf_op jit(solution)/shard_map/all_gather | solution.py:90
  52.1 38.8 %all_gather.24 = bf16[768,3,192]{2,0,1:T(8,128)(2,1)S(1)} all-gather(bf16[24,3,192]{2,0,1:T(8,128)(2,1)S(1)} %copy-done.41), channel_id=1, replica_groups=mesh['shard'=2,'context'=16,'tensor'=4] {'shard','context'}, dimensions={0}, use_global_device_ids=true | all-gather | bytes 912384 | tf_op jit(solution)/shard_map/all_gather | solution.py:86
  97.1 40.7 %all_gather.27 = bf16[768,192]{1,0:T(8,128)(2,1)S(1)} all-gather(bf16[24,192]{1,0:T(8,128)(2,1)S(1)} %copy-done.46), channel_id=1, replica_groups=mesh['shard'=2,'context'=16,'tensor'=4] {'shard','context'}, dimensions={0}, use_global_device_ids=true | all-gather | bytes 304128 | tf_op jit(solution)/shard_map/all_gather | solution.py:87
  139.5 6.2 all-gather.7.cloned.1.call-done
  145.7 51.8 %all-gather.13.cloned.1.call-done = bf16[1,6144,1,192]{1,3,2,0:T(8,128)(2,1)} async-done(((bf16[1,384,1,192]{1,3,2,0:T(8,128)(2,1)}), bf16[1,6144,1,192]{1,3,2,0:T(8,128)(2,1)}) %all-gather.13.cloned.1.call-update) | async-done | bytes 2359312 | tf_op jit(solution)/shard_map/all_gather | solution.py:133
  197.6 67.3 %while.36 = (s32[]{:T(128)}, f32[1,3,384]{2,1,0:T(4,128)S(1)}, f32[1,3,384]{2,1,0:T(4,128)S(1)}, f32[1,3,384,64]{2,3,1,0:T(8,128)S(1)}, s32[1,6144]{1,0:T(1,128)...) while((s32[]{:T(128)}, f32[1,3,384]{2,1,0:T(4,128)S(1)}, ...), condition=%wide.region_5.6_spmd.clone, body=%wide.region_2.5_spmd.clone.sunk | while | flops 534805248 | bytes 9865923 | solution.py:164
  265.5 2.2 multiply_reduce_fusion.7
  267.7 2.7 broadcast_in_dim.99
  270.4 2.7 broadcast_in_dim.99.clone
  273.1 152.7 %while.37 = (s32[]{:T(128)}, f32[1,3,384,64]{2,3,1,0:T(8,128)}, f32[1,6144,3,64]{1,3,2,0:T(8,128)}, f32[1,6144,3,64]{1,3,2,0:T(8,128)}, s32[1,6144]{1,0:T(1,128)...) while((s32[]{:T(128)}, f32[1,3,384,64]{2,3,1,0:T(8,128)}, ...), condition=%wide.region_9.10_spmd.clone, body=%wide.region_8.9_spmd.clone.sunk | while | flops 384319488 | bytes 15361789 | solution.py:268
  279.2 2.2 fusion.141
  281.4 2.4 fusion.142
  291.8 2.2 fusion.141
  294.0 2.3 fusion.142
  306.7 2.4 fusion.142
  317.3 2.2 fusion.141
  319.5 2.4 fusion.142
  330.1 2.2 fusion.141
  332.3 2.3 fusion.142
  345.0 2.3 fusion.142
  357.7 2.3 fusion.142
  370.4 2.3 fusion.142
  380.9 2.2 fusion.141
  383.1 2.4 fusion.142
  393.7 2.2 fusion.141
  395.9 2.4 fusion.142
  406.4 2.2 fusion.141
  408.6 2.3 fusion.142
  419.2 2.2 fusion.141
  421.3 2.3 fusion.142
  427.1 5.4 fusion.43
  432.5 3.1 fusion.76
  438.0 67.5 %reduce-scatter.12.cloned.1.call-done = f32[1,384,192]{1,2,0:T(8,128)} async-done(((f32[1,6144,192]{1,2,0:T(8,128)}), f32[1,384,192]{1,2,0:T(8,128)}) %reduce-scatter.12.cloned.1.call-update) | async-done | bytes 294928 | tf_op jit(solution)/shard_map/reduce_scatter | solution.py:272
  508.4 82.6 %reduce-scatter.14.cloned.1.call-done = f32[1,384,192]{1,2,0:T(8,128)} async-done(((f32[1,6144,192]{1,2,0:T(8,128)}), f32[1,384,192]{1,2,0:T(8,128)}) %reduce-scatter.14.cloned.1.call-update) | async-done | bytes 294928 | tf_op jit(solution)/shard_map/reduce_scatter | solution.py:278
  592.7 3.0 convolution_bitcast_fusion.5
  600.0 2.2 copy.69
  602.3 2.4 fusion.61
  604.7 2.3 convolution_bitcast_fusion.3
  607.0 3.1 copy.71
  611.1 2.4 fusion.64
  616.9 42.4 %all-reduce.8.cloned.1.call-done = (f32[1,384,768]{2,1,0:T(8,128)}, f32[1,384,768]{2,1,0:T(8,128)}) async-done(((f32[1,384,768]{2,1,0:T(8,128)}, f32[1,384,768]{2,1,0:T(8,128)}), (f32[1,384,768]{2,1,0:T(8,128)}, f32[1,384,768]{2,1,0:T(8,128)})) %all-reduce.8.cloned.1.call-update) | async-done | bytes 2359312 | tf_op jit(solution)/shard_map/psum | solution.py:309
  659.4 3.3 multiply_reduce_fusion
  666.4 123.4 %all-reduce.1 = (f32[768,6]{0,1:T(8,128)}, f32[3,192]{1,0:T(4,128)}, f32[768]{0:T(1024)}) all-reduce(f32[768,6]{0,1:T(8,128)} %concatenate.36, f32[3,192]{1,0:T(4,128)} %maximum_reduce_fusion, f32[768]{0:T(1024)} %get-tuple-element.606), channel_id=5, replica_groups=mesh['shard'=2,'context'=16,'tensor'=4] {'shard','context'}, use_global_device_ids=true, to_apply=%region_23.24.clone | all-reduce | flops 5952 | bytes 47616
  796.0 3.5 multiply_add_fusion
  799.5 39.7 %reduce-scatter.20.cloned.1.call-done = f32[24,192]{1,0:T(8,128)} async-done(((f32[768,192]{1,0:T(8,128)}), f32[24,192]{1,0:T(8,128)}) %reduce-scatter.20.cloned.1.call-update) | async-done | bytes 18448
  839.2 137.4 %reduce-scatter.18.cloned.1.call-done = f32[24,768]{1,0:T(8,128)} async-done(((f32[768,768]{1,0:T(8,128)}), f32[24,768]{1,0:T(8,128)}) %reduce-scatter.18.cloned.1.call-update) | async-done | bytes 73744 | tf_op jit(solution)/shard_map/reduce_scatter | solution.py:331
  976.6 137.9 %reduce-scatter.22.cloned.1.call-done = f32[24,768]{1,0:T(8,128)} async-done(((f32[768,768]{1,0:T(8,128)}), f32[24,768]{1,0:T(8,128)}) %reduce-scatter.22.cloned.1.call-update) | async-done | bytes 73744
  1114.4 137.5 %reduce-scatter.16.cloned.1.call-done = f32[24,3,192]{2,0,1:T(8,128)} async-done(((f32[768,3,192]{2,0,1:T(8,128)}), f32[24,3,192]{2,0,1:T(8,128)}) %reduce-scatter.16.cloned.1.call-update) | async-done | bytes 55312 | tf_op jit(solution)/shard_map/reduce_scatter | solution.py:325
  (420 shorter events, 210.5 us)
Async XLA Ops:
  7.2 1.7 copy-start.1
  7.2 138.6 %all-gather.7.cloned.1.call-start = ((), (), s32[]{:S(2)}) async-start(), calls=%async_computation.6 | async-start | bytes 2506752 | tf_op jit(solution)/shard_map/all_gather | solution.py:132
  7.3 1.9 copy-start.47
  7.3 1.9 copy-start.48
  7.3 1.9 copy-start.49
  7.3 1.9 copy-start.50
  7.3 1.9 copy-start.51
  7.3 1.9 copy-start.52
  7.3 44.8 %copy-start.41 = (bf16[24,3,192]{2,0,1:T(8,128)(2,1)S(1)}, bf16[24,3,192]{2,0,1:T(8,128)(2,1)}, u32[]{:S(2)}) copy-start(bf16[24,3,192]{2,0,1:T(8,128)(2,1)} %param.25) | copy-start | bytes 82948
  8.9 82.0 %copy-start.31 = (f32[384]{0:T(512)}, f32[384]{0:T(512)S(1)}, u32[]{:S(2)}) copy-start(f32[384]{0:T(512)S(1)} %broadcast_multiply_fusion.5) | copy-start | bytes 4612
  8.9 82.0 %copy-start.53 = (f32[3,192]{1,0:T(4,128)S(1)}, f32[3,192]{1,0:T(4,128)}, u32[]{:S(2)}) copy-start(f32[3,192]{1,0:T(4,128)} %param.26) | copy-start | bytes 6916
  9.1 81.7 %copy-start.37 = (f32[384]{0:T(512)}, f32[384]{0:T(512)S(1)}, u32[]{:S(2)}) copy-start(f32[384]{0:T(512)S(1)} %add_rsqrt_fusion) | copy-start | bytes 4612
  52.1 38.8 %copy-start.35 = (f32[768]{0:T(1024)}, f32[768]{0:T(1024)S(1)}, u32[]{:S(2)}) copy-start(f32[768]{0:T(1024)S(1)} %get-tuple-element.517) | copy-start | bytes 9220
  52.1 38.8 %copy-start.42 = (f32[768]{0:T(1024)}, f32[768]{0:T(1024)S(1)}, u32[]{:S(2)}) copy-start(f32[768]{0:T(1024)S(1)} %get-tuple-element.516) | copy-start | bytes 9220
  91.9 4.5 copy-start.6
  94.2 103.4 %all-gather.13.cloned.1.call-start = ((), (), s32[]{:S(2)}) async-start(), calls=%async_computation.14 | async-start | bytes 2506752 | tf_op jit(solution)/shard_map/all_gather | solution.py:133
  94.9 2.2 copy-start.46
  95.0 331.6 %all-gather.9.cloned.1.call-start = ((), (), s32[]{:S(2)}) async-start(), calls=%async_computation.7 | async-start | bytes 1216512 | tf_op jit(solution)/shard_map/all_gather | solution.py:88
  95.7 336.8 %all-gather.11.cloned.1.call-start = ((), (), s32[]{:S(2)}) async-start(), calls=%async_computation.8 | async-start | bytes 1216512 | tf_op jit(solution)/shard_map/all_gather | solution.py:89
  96.3 409.3 %reduce-scatter.12.cloned.1.call-start = ((), (), s32[]{:S(2)}) async-start(), calls=%async_computation.10 | async-start | bytes 5013504 | tf_op jit(solution)/shard_map/reduce_scatter | solution.py:272
  97.1 40.7 %copy-start.4 = (bf16[1,384,768]{2,1,0:T(8,128)(2,1)}, bf16[1,384,768]{2,1,0:T(8,128)(2,1)S(1)}, u32[]{:S(2)}) copy-start(bf16[1,384,768]{2,1,0:T(8,128)(2,1)S(1)} %get-tuple-element.578) | copy-start | bytes 1769476
  325.7 1.5 copy-start
  425.8 165.3 %reduce-scatter.14.cloned.1.call-start = ((), (), s32[]{:S(2)}) async-start(), calls=%async_computation.11 | async-start | bytes 5013504 | tf_op jit(solution)/shard_map/reduce_scatter | solution.py:278
  426.3 233.0 %all-reduce.8.cloned.1.call-start = ((), (), s32[]{:S(2)}) async-start(), calls=%async_computation.17 | async-start | bytes 4718592 | tf_op jit(solution)/shard_map/psum | solution.py:309
  427.1 5.4 copy-start.5
  432.5 3.1 copy-start.18
  435.6 1.7 copy-start.3
  435.6 70.9 %copy-start.40 = (f32[384,8]{0,1:T(8,128)S(1)}, f32[384,8]{0,1:T(8,128)}, u32[]{:S(2)}) copy-start(f32[384,8]{0,1:T(8,128)} %get-tuple-element.601) | copy-start | bytes 36868
  507.4 88.3 %copy-start.25 = (f32[1,384,3,8]{1,3,2,0:T(8,128)}, f32[1,384,3,8]{1,3,2,0:T(8,128)S(1)}, u32[]{:S(2)}) copy-start(f32[1,384,3,8]{1,3,2,0:T(8,128)S(1)} %get-tuple-element.584) | copy-start | bytes 110596
  507.4 88.3 %copy-start.27 = (f32[1,384,3,8]{1,3,2,0:T(8,128)}, f32[1,384,3,8]{1,3,2,0:T(8,128)S(1)}, u32[]{:S(2)}) copy-start(f32[1,384,3,8]{1,3,2,0:T(8,128)S(1)} %get-tuple-element.591) | copy-start | bytes 110596
  507.4 88.3 %copy-start.29 = (f32[1,384,3,8]{1,3,2,0:T(8,128)}, f32[1,384,3,8]{1,3,2,0:T(8,128)S(1)}, u32[]{:S(2)}) copy-start(f32[1,384,3,8]{1,3,2,0:T(8,128)S(1)} %get-tuple-element.592) | copy-start | bytes 110596
  508.4 87.3 %copy-start.19 = (bf16[1,384,3,64]{1,3,2,0:T(8,128)(2,1)}, bf16[1,384,3,64]{1,3,2,0:T(8,128)(2,1)S(1)}, u32[]{:S(2)}) copy-start(bf16[1,384,3,64]{1,3,2,0:T(8,128)(2,1)S(1)} %get-tuple-element.610) | copy-start | bytes 442372
  508.4 87.3 %copy-start.21 = (bf16[1,384,3,64]{1,3,2,0:T(8,128)(2,1)}, bf16[1,384,3,64]{1,3,2,0:T(8,128)(2,1)S(1)}, u32[]{:S(2)}) copy-start(bf16[1,384,3,64]{1,3,2,0:T(8,128)(2,1)S(1)} %get-tuple-element.611) | copy-start | bytes 442372
  595.8 200.2 %all-reduce.6.cloned.1.call-start = ((), (), s32[]{:S(2)}) async-start(), calls=%async_computation.9 | async-start | bytes 1179648 | tf_op jit(solution)/shard_map/psum | solution.py:182
  598.8 240.4 %reduce-scatter.20.cloned.1.call-start = ((), (), s32[]{:S(2)}) async-start(), calls=%async_computation.15 | async-start | bytes 811008
  602.2 374.4 %reduce-scatter.18.cloned.1.call-start = ((), (), s32[]{:S(2)}) async-start(), calls=%async_computation.13 | async-start | bytes 2433024 | tf_op jit(solution)/shard_map/reduce_scatter | solution.py:331
  604.7 509.8 %reduce-scatter.22.cloned.1.call-start = ((), (), s32[]{:S(2)}) async-start(), calls=%async_computation.16 | async-start | bytes 2433024
  610.1 641.9 %reduce-scatter.16.cloned.1.call-start = ((), (), s32[]{:S(2)}) async-start(), calls=%async_computation.12 | async-start | bytes 2433024 | tf_op jit(solution)/shard_map/reduce_scatter | solution.py:325
  613.5 2.5 copy-start.11
  613.5 2.5 copy-start.13
  613.5 2.5 copy-start.26
  613.6 2.5 copy-start.28
  613.6 2.5 copy-start.30
  613.6 2.6 copy-start.16
  613.6 45.8 %copy-start.34 = (f32[768]{0:T(1024)S(1)}, f32[768]{0:T(1024)}, u32[]{:S(2)}) copy-start(f32[768]{0:T(1024)} %get-tuple-element.515) | copy-start | bytes 9220
  613.6 45.8 %copy-start.39 = (f32[384]{0:T(512)S(1)}, f32[384]{0:T(512)}, u32[]{:S(2)}) copy-start(f32[384]{0:T(512)} %copy-done.37) | copy-start | bytes 4612
  659.4 136.6 %copy-start.7 = (f32[1,384,768]{2,1,0:T(8,128)S(1)}, f32[1,384,768]{2,1,0:T(8,128)}, u32[]{:S(2)}) copy-start(f32[1,384,768]{2,1,0:T(8,128)} %param.33) | copy-start | bytes 3538948
  659.4 136.6 %copy-start.8 = (f32[1,384,768]{2,1,0:T(8,128)S(1)}, f32[1,384,768]{2,1,0:T(8,128)}, u32[]{:S(2)}) copy-start(f32[1,384,768]{2,1,0:T(8,128)} %get-tuple-element.563) | copy-start | bytes 3538948
  (31 other events, 38.2 us)
Sparse Core Ops, SparseCore 0:
  94.3 51.3 all-gather.6
  148.0 49.5 all-gather.12
  199.3 54.4 all-gather.8
  255.3 55.1 all-gather.10
  425.9 79.5 reduce-scatter.11
  509.4 81.5 reduce-scatter.13
  595.9 63.4 all-reduce.7
  662.3 41.2 all-reduce.5
  706.5 132.6 reduce-scatter.19
  842.0 134.5 reduce-scatter.17
  979.5 134.8 reduce-scatter.21
  1117.3 134.6 reduce-scatter.15
where the time goes:
time: 1270 us; the launch traced here: 1260 us
  waiting for transfers between devices  705 us (56%)
  blocking collectives  245 us (19%)
  matrix products  183 us (14%)
  local copies, waits for them, and re-layouts  73.6 us (6%)
  other arithmetic  35.4 us (3%)
  between operations  15.5 us (1%)
    unnamed x14, waiting for transfers between devices  179 us
    reduce_scatter x1, waiting for transfers between devices, shards(): lax.psum_scatter(query_key_value_weight_gradient, ('shard', 'context'), s...  138 us
    reduce_scatter x1, waiting for transfers between devices, shards(): lax.psum_scatter(up_weight_gradient, ('shard', 'context'), scatter_dimens...  137 us
    unnamed x1, blocking collectives  123 us
    reduce_scatter x1, waiting for transfers between devices, shards(): lax.psum_scatter(grad_val.reshape(seqs_here, full_len, inner_here), 'cont...  82.6 us
    reduce_scatter x1, waiting for transfers between devices, shards(): lax.psum_scatter(grad_key.reshape(seqs_here, full_len, inner_here), 'cont...  67.5 us
    all_gather x1, waiting for transfers between devices, shards(): val_piece = lax.all_gather(values_flat, 'context', axis=1, tiled=True)  51.8 us
    psum x1, waiting for transfers between devices, shards(): lax.psum((norm1_output_gradient, norm2_output_gradient), 'tensor')  42.4 us
  transfers between devices with their start and end apart: 12, of which 9 were waited for; matrix products, arithmetic and copies ran while one was open for 22% of the time, Pallas kernels for 0%

commit v1 on v0

v1 whole, which is shorter than its diff:
```python
import functools
import math

import jax
import jax.numpy as jnp
from jax import lax
from jax.experimental import pallas as pl
from jax.experimental.pallas import tpu as pltpu
from jax.sharding import PartitionSpec as P

HS = 64
ROT = 16
BF = jnp.bfloat16
F32 = jnp.float32
MESH = pl.DeviceIdType.MESH
norm_eps = 1e-05


def coords():
    s = lax.axis_index("shard")
    c = lax.axis_index("context")
    z = lax.axis_index("tensor")
    x = lax.div(c, 4)
    yh = lax.rem(lax.div(c, 2), 2)
    k = lax.rem(c, 2)
    return x, yh * 2 + s, k, z


def dev(x, y, k, z):
    return (lax.rem(y, 2), x * 4 + lax.div(y, 2) * 2 + k, z)


def m4(a):
    return lax.rem(a, 4)


class Mail:
    def __init__(self, send_sems, recv_sems):
        self.send_sems, self.recv_sems, self.made = send_sems, recv_sems, []

    def send(self, src, dst, device):
        i = len(self.made)
        assert i < self.send_sems.shape[0]
        copy = pltpu.make_async_remote_copy(
            src_ref=src,
            dst_ref=dst,
            send_sem=self.send_sems.at[i],
            recv_sem=self.recv_sems.at[i],
            device_id=device,
            device_id_type=MESH,
        )
        copy.start()
        self.made.append(copy)
        return i

    def recv(self, i):
        self.made[i].wait_recv()

    def close(self):
        for copy in self.made:
            copy.wait_send()


def greet(devices):
    barrier = pltpu.get_barrier_semaphore()
    for device in devices:
        pl.semaphore_signal(barrier, inc=1, device_id=device, device_id_type=MESH)
    pl.semaphore_wait(barrier, len(devices))


def comm_call(kernel, name, cid, n_copies, outs, scratch, args, in_vmem=None, out_vmem=None):
    anyspec = pl.BlockSpec(memory_space=pl.ANY)
    vspec = pl.BlockSpec(memory_space=pltpu.VMEM)
    in_vmem = in_vmem or [False] * len(args)
    out_vmem = out_vmem or [False] * len(outs)
    return pl.pallas_call(
        kernel,
        name=name,
        out_shape=[jax.ShapeDtypeStruct(*o) for o in outs],
        in_specs=[vspec if v else anyspec for v in in_vmem],
        out_specs=[vspec if v else anyspec for v in out_vmem],
        scratch_shapes=list(scratch)
        + [
            pltpu.SemaphoreType.DMA((n_copies,)),
            pltpu.SemaphoreType.DMA((n_copies,)),
            pltpu.SemaphoreType.DMA((4,)),
        ],
        compiler_params=pltpu.CompilerParams(
            collective_id=cid, has_side_effects=True, vmem_limit_bytes=56 * 1024 * 1024
        ),
    )(*args)


WCOLS = 2432
P_CUT = (0, 640, 1280)
Q_CUT = (1280, 1792, 2432)


def gather_weights_kernel(src, out, ss, rs, ls):
    x, y, k, z = coords()
    mail = Mail(ss, rs)

    def row(xx, yy):
        return lax.rem(yy, 2) * 16 + xx * 4 + lax.div(yy, 2) * 2 + k

    xs = [x, m4(x + 3), m4(x + 1), m4(x + 2)]
    ys = [y, m4(y + 3), m4(y + 1), m4(y + 2)]
    mate = dev(x, y, 1 - k, z)
    step = {
        "x": (dev(xs[2], y, k, z), dev(xs[1], y, k, z)),
        "y": (dev(x, ys[2], k, z), dev(x, ys[1], k, z)),
    }
    greet([step["x"][0], step["x"][1], step["y"][0], step["y"][1], mate])
    me = row(x, y)
    own = pltpu.make_async_copy(src, out.at[me], ls.at[0])
    own.start()

    def part(r, lo, hi):
        return out.at[r, :, pl.ds(lo, hi - lo)]

    def begin(view, r, cut, axis):
        return [
            mail.send(view, part(r, cut[0], cut[2]), step[axis][0]),
            mail.send(view, part(r, cut[0], cut[2]), step[axis][1]),
        ]

    def own_view(cut):
        return src.at[:, pl.ds(cut[0], cut[2] - cut[0])]

    mates = []

    def to_mate(r, lo, hi):
        mates.append(mail.send(part(r, lo, hi), part(r, lo, hi), mate))

    plans = [("x", "y", P_CUT), ("y", "x", Q_CUT)]
    first = [begin(own_view(cut), me, cut, a) for a, b, cut in plans]
    second = [[begin(own_view(cut), me, cut, b)] for a, b, cut in plans]
    mates.append(mail.send(src, out.at[me], mate))

    def at(a, i, j):
        return row(xs[i], ys[j]) if a == "x" else row(xs[j], ys[i])

    relays = [[], []]
    for i in (1, 2):
        for n, (a, b, cut) in enumerate(plans):
            mail.recv(first[n][i - 1])
            r = at(a, i, 0)
            lo, hi = (cut[0], cut[1]) if i == 1 else (cut[1], cut[2])
            relays[n].append(mail.send(part(r, lo, hi), part(r, lo, hi), step[a][i - 1]))
            second[n].append(begin(part(r, cut[0], cut[2]), r, cut, b))
            to_mate(r, cut[0], cut[2])
    for n, (a, b, cut) in enumerate(plans):
        for i in relays[n]:
            mail.recv(i)
        r = at(a, 3, 0)
        second[n].append(begin(part(r, cut[0], cut[2]), r, cut, b))
        to_mate(r, cut[0], cut[2])
    late = []
    for i in range(4):
        for n, (a, b, cut) in enumerate(plans):
            pair = []
            for j in (1, 2):
                mail.recv(second[n][i][j - 1])
                r = at(a, i, j)
                lo, hi = (cut[0], cut[1]) if j == 1 else (cut[1], cut[2])
                pair.append(mail.send(part(r, lo, hi), part(r, lo, hi), step[b][j - 1]))
                to_mate(r, cut[0], cut[2])
            late.append((pair, at(a, i, 3), cut))
    for pair, r, cut in late:
        for i in pair:
            mail.recv(i)
        to_mate(r, cut[0], cut[2])
    for i in mates:
        mail.recv(i)
    own.wait()
    mail.close()


def gather_weights(src):
    return comm_call(
        gather_weights_kernel, "gather_weights", 1, 80,
        [((32, 24, WCOLS), BF)], [], [src],
    )[0]


def spread_z(mail, z, x, y, k, src, dst):
    made = []
    for d in (1, 3, 2):
        peer = m4(z + d)
        made.append(mail.send(src.at[peer], dst.at[z], dev(x, y, k, peer)))
    return made


def gather_attention_kernel(a_ref, kv_ref, n2_ref, a_out, kv_out, n2_out, relay, ss, rs, ls):
    x, y, k, z = coords()
    mail = Mail(ss, rs)
    xl, xr = m4(x + 3), m4(x + 1)
    right, left = dev(xr, y, k, z), dev(xl, y, k, z)
    up, down = dev(x, m4(y + 1), k, z), dev(x, m4(y + 3), k, z)
    mate = dev(x, y, 1 - k, z)
    greet([right, left, up, down, mate] + [dev(x, y, k, m4(z + d)) for d in (1, 2, 3)])
    slot = lax.div(y, 2) * 2 + k
    far = (1 - lax.div(y, 2)) * 2 + k
    top, low = pl.ds(0, 192), pl.ds(192, 192)
    y1 = mail.send(kv_ref.at[top], relay.at[0], up)
    y2 = mail.send(kv_ref.at[low], relay.at[1], down)
    x1 = mail.send(a_ref, a_out.at[x], right)
    x2 = mail.send(a_ref, a_out.at[x], left)
    c1 = mail.send(kv_ref, kv_out.at[slot], mate)
    zs = spread_z(mail, z, x, y, k, n2_ref, n2_out)
    locals_ = [
        pltpu.make_async_copy(a_ref, a_out.at[x], ls.at[0]),
        pltpu.make_async_copy(kv_ref, kv_out.at[slot], ls.at[1]),
        pltpu.make_async_copy(n2_ref.at[z], n2_out.at[z], ls.at[2]),
    ]
    for copy in locals_:
        copy.start()
    up_slot = lax.div(m4(y + 3), 2) * 2 + k
    down_slot = lax.div(m4(y + 1), 2) * 2 + k
    mail.recv(y1)
    y3 = mail.send(relay.at[0], kv_out.at[up_slot, top], up)
    mail.recv(y2)
    y4 = mail.send(relay.at[1], kv_out.at[down_slot, low], down)
    mail.recv(x1)
    x3 = mail.send(a_out.at[xl, top], a_out.at[xl, top], right)
    mail.recv(x2)
    x4 = mail.send(a_out.at[xr, low], a_out.at[xr, low], left)
    mail.recv(y3)
    mail.recv(y4)
    c2 = mail.send(kv_out.at[far], kv_out.at[far], mate)
    for i in [x3, x4, c1, c2] + zs:
        mail.recv(i)
    for copy in locals_:
        copy.wait()
    mail.close()


def gather_attention(a, kv, n2):
    return comm_call(
        gather_attention_kernel, "gather_attention", 2, 16,
        [((4, 384, 384), BF), ((4, 384, 384), BF), ((4, 96, 768), BF)],
        [pltpu.VMEM((2, 192, 384), BF)],
        [a, kv, n2],
    )


def exchange_x(mail, x, y, k, z, src, dst, relay):
    xl, xr, xo = m4(x + 3), m4(x + 1), m4(x + 2)
    right, left = dev(xr, y, k, z), dev(xl, y, k, z)
    top, low = pl.ds(0, 96), pl.ds(96, 96)
    r1 = mail.send(src.at[xo, top], relay.at[0], right)
    r2 = mail.send(src.at[xo, low], relay.at[1], left)
    made = [
        mail.send(src.at[xr], dst.at[x], right),
        mail.send(src.at[xl], dst.at[x], left),
    ]

    def finish():
        mail.recv(r1)
        made.append(mail.send(relay.at[0], dst.at[xl, top], right))
        mail.recv(r2)
        made.append(mail.send(relay.at[1], dst.at[xr, low], left))
        return made

    return finish


def share_partials_kernel(o_ref, st_ref, o_out, st_out, relay, ss, rs, ls):
    x, y, k, z = coords()
    mail = Mail(ss, rs)
    greet([dev(m4(x + d), y, k, z) for d in (1, 2, 3)])
    made = [mail.send(st_ref, st_out.at[x], dev(m4(x + d), y, k, z)) for d in (1, 3, 2)]
    finish = exchange_x(mail, x, y, k, z, o_ref, o_out, relay)
    own = [
        pltpu.make_async_copy(o_ref.at[x], o_out.at[x], ls.at[0]),
        pltpu.make_async_copy(st_ref, st_out.at[x], ls.at[1]),
    ]
    for copy in own:
        copy.start()
    for i in finish() + made:
        mail.recv(i)
    for copy in own:
        copy.wait()
    mail.close()


def share_partials(o, st):
    return comm_call(
        share_partials_kernel, "share_partials", 3, 12,
        [((4, 192, 384), BF), ((4, 8, 1536), F32)],
        [pltpu.VMEM((2, 96, 384), BF)],
        [o, st],
    )


def reduce_attention_kernel(
    dq_ref, dkv_ref, br_ref, dq_out, dkv_out, br_out,
    relay_x, relay_y, mate_in, summed, far_in, z_in, z_sum, ss, rs, ls,
):
    x, y, k, z = coords()
    mail = Mail(ss, rs)
    up, down = dev(x, m4(y + 1), k, z), dev(x, m4(y + 3), k, z)
    mate = dev(x, y, 1 - k, z)
    greet(
        [dev(m4(x + 1), y, k, z), dev(m4(x + 3), y, k, z), up, down, mate]
        + [dev(x, y, k, m4(z + d)) for d in (1, 2, 3)]
    )
    yh = lax.div(y, 2)
    far = 1 - yh
    c1 = mail.send(dkv_ref.at[far * 2 + 1 - k], mate_in.at[0], mate)
    c2 = mail.send(dkv_ref.at[yh * 2 + 1 - k], mate_in.at[1], mate)
    zs = spread_z(mail, z, x, y, k, br_ref, z_in)
    finish = exchange_x(mail, x, y, k, z, dq_ref, dq_out, relay_x)
    own = pltpu.make_async_copy(dq_ref.at[x], dq_out.at[x], ls.at[0])
    own.start()
    mail.recv(c1)
    summed[...] = (dkv_ref[far * 2 + k].astype(F32) + mate_in[0].astype(F32)).astype(BF)
    top, low = pl.ds(0, 192), pl.ds(192, 192)
    y1 = mail.send(summed.at[top], relay_y.at[0], up)
    y2 = mail.send(summed.at[low], relay_y.at[1], down)
    mail.recv(c2)
    dkv_out[...] = dkv_ref[yh * 2 + k].astype(F32) + mate_in[1].astype(F32)
    for i in zs:
        mail.recv(i)
    total = br_ref[z].astype(F32)
    for d in (1, 2, 3):
        total = total + z_in[m4(z + d)].astype(F32)
    z_sum[...] = total.astype(BF)
    made = [mail.send(z_sum, br_out.at[z], dev(x, y, k, m4(z + d))) for d in (1, 3, 2)]
    own_z = pltpu.make_async_copy(z_sum, br_out.at[z], ls.at[1])
    own_z.start()
    mail.recv(y1)
    y3 = mail.send(relay_y.at[0], far_in.at[top], up)
    mail.recv(y2)
    y4 = mail.send(relay_y.at[1], far_in.at[low], down)
    made += finish()
    mail.recv(y3)
    mail.recv(y4)
    dkv_out[...] += far_in[...].astype(F32)
    for i in made:
        mail.recv(i)
    own.wait()
    own_z.wait()
    mail.close()


def reduce_attention(dq, dkv, br):
    return comm_call(
        reduce_attention_kernel, "reduce_attention", 4, 24,
        [((4, 192, 384), BF), ((384, 384), F32), ((4, 96, 768), BF)],
        [
            pltpu.VMEM((2, 96, 384), BF),
            pltpu.VMEM((2, 192, 384), BF),
            pltpu.VMEM((2, 384, 384), BF),
            pltpu.VMEM((384, 384), BF),
            pltpu.VMEM((384, 384), BF),
            pltpu.VMEM((4, 96, 768), BF),
            pltpu.VMEM((96, 768), BF),
        ],
        [dq, dkv, br],
        [False, True, True],
        [False, True, False],
    )


GCOLS = 2304
GHALF = 1152


def reduce_weights_kernel(
    g_ref, n1_ref, w_out, n1_out,
    mate_in, e, relay1, fwd1, in1, f, relay2, fwd2, in2, ss, rs, ls,
):
    x, y, k, z = coords()
    mail = Mail(ss, rs)
    mate = dev(x, y, 1 - k, z)
    step = [
        (dev(m4(x + 1), y, k, z), dev(m4(x + 3), y, k, z)),
        (dev(x, m4(y + 1), k, z), dev(x, m4(y + 3), k, z)),
    ]
    greet(list(step[0] + step[1]) + [mate] + [dev(x, y, k, m4(z + d)) for d in (1, 2, 3)])
    cs = []
    for n in range(2):
        cs.append(mail.send(g_ref.at[1 - k, n], mate_in.at[n], mate))
    zs = spread_z(mail, z, x, y, k, n1_ref, n1_out)
    own = pltpu.make_async_copy(n1_ref.at[z], n1_out.at[z], ls.at[0])
    own.start()
    pos = (x, y)
    r1 = []
    plain = []
    for n in range(2):
        a = pos[n]
        mail.recv(cs[n])

        def add(i, _):
            e[n, i] = (g_ref[k, n, i].astype(F32) + mate_in[n, i].astype(F32)).astype(BF)
            return 0

        lax.fori_loop(0, 4, add, 0)
        opp = m4(a + 2)
        r1.append(
            (
                mail.send(e.at[n, opp, pl.ds(0, 2)], relay1.at[n, 0], step[n][0]),
                mail.send(e.at[n, opp, pl.ds(2, 2)], relay1.at[n, 1], step[n][1]),
            )
        )
        plain.append(
            (
                mail.send(e.at[n, m4(a + 1), pl.ds(2, 2)], in1.at[n, 0, pl.ds(2, 2)], step[n][0]),
                mail.send(e.at[n, m4(a + 3), pl.ds(0, 2)], in1.at[n, 1, pl.ds(0, 2)], step[n][1]),
            )
        )
    more = []
    for n in range(2):
        a = pos[n]
        mail.recv(r1[n][0])
        fwd1[n, 0] = (
            e[n, m4(a + 1), pl.ds(0, 2)].astype(F32) + relay1[n, 0].astype(F32)
        ).astype(BF)
        m1 = mail.send(fwd1.at[n, 0], in1.at[n, 0, pl.ds(0, 2)], step[n][0])
        mail.recv(r1[n][1])
        fwd1[n, 1] = (
            e[n, m4(a + 3), pl.ds(2, 2)].astype(F32) + relay1[n, 1].astype(F32)
        ).astype(BF)
        m2 = mail.send(fwd1.at[n, 1], in1.at[n, 1, pl.ds(2, 2)], step[n][1])
        more.append((m1, m2))
    r2 = []
    plain2 = []
    c0, c1 = pl.ds(0, 640), pl.ds(640, 512)
    for n in range(2):
        a, b = pos[n], pos[1 - n]
        for i in plain[n] + more[n]:
            mail.recv(i)
        f[n] = (
            e[n, a].astype(F32) + in1[n, 0].astype(F32) + in1[n, 1].astype(F32)
        ).astype(BF)
        go = step[1 - n]
        r2.append(
            (
                mail.send(f.at[n, m4(b + 2), :, c0], relay2.at[n, :, c0], go[0]),
                mail.send(f.at[n, m4(b + 2), :, c1], relay2.at[n, :, c1], go[1]),
            )
        )
        plain2.append(
            (
                mail.send(f.at[n, m4(b + 1), :, c1], in2.at[n, 0, :, c1], go[0]),
                mail.send(f.at[n, m4(b + 3), :, c0], in2.at[n, 1, :, c0], go[1]),
            )
        )
    more2 = []
    for n in range(2):
        b = pos[1 - n]
        go = step[1 - n]
        mail.recv(r2[n][0])
        fwd2[n, :, c0] = (
            f[n, m4(b + 1), :, c0].astype(F32) + relay2[n, :, c0].astype(F32)
        ).astype(BF)
        m1 = mail.send(fwd2.at[n, :, c0], in2.at[n, 0, :, c0], go[0])
        mail.recv(r2[n][1])
        fwd2[n, :, c1] = (
            f[n, m4(b + 3), :, c1].astype(F32) + relay2[n, :, c1].astype(F32)
        ).astype(BF)
        m2 = mail.send(fwd2.at[n, :, c1], in2.at[n, 1, :, c1], go[1])
        more2.append((m1, m2))
    for n in range(2):
        b = pos[1 - n]
        for i in plain2[n] + more2[n]:
            mail.recv(i)
        w_out[n] = f[n, b].astype(F32) + in2[n, 0].astype(F32) + in2[n, 1].astype(F32)
    for i in zs:
        mail.recv(i)
    own.wait()
    mail.close()


def reduce_weights(g, n1):
    def buf(*lead):
        return pltpu.VMEM(lead + (24, GHALF), BF)

    return comm_call(
        reduce_weights_kernel, "reduce_weights", 5, 29,
        [((2, 24, GHALF), F32), ((4, 96, 768), BF)],
        [
            buf(2, 4, 4), buf(2, 4, 4), buf(2, 2, 2), buf(2, 2, 2), buf(2, 2, 4),
            buf(2, 4), buf(2), buf(2), buf(2, 2),
        ],
        [g, n1],
        [True, False],
        [True, False],
    )


def finish_kernel(p_ref, v_ref, p_out, v_out, cin, xin, yin, zin, t1, t2, t3, ss, rs, ls):
    x, y, k, z = coords()
    mail = Mail(ss, rs)
    mate = dev(x, y, 1 - k, z)
    xs = [dev(m4(x + d), y, k, z) for d in (1, 3, 2)]
    ys = [dev(x, m4(y + d), k, z) for d in (1, 3, 2)]
    zs = [dev(x, y, k, m4(z + d)) for d in (1, 3, 2)]
    greet([mate] + xs + ys + zs)
    c = mail.send(v_ref, cin, mate)
    ps = [mail.send(p_ref, p_out.at[z], d) for d in zs]
    own = pltpu.make_async_copy(p_ref, p_out.at[z], ls.at[0])
    own.start()
    mail.recv(c)
    t1[...] = v_ref[...] + cin[...]

    def stage(mine, slots, me, peers):
        made = [mail.send(mine, slots.at[me], d) for d in peers]
        slots[me] = mine[...]
        for i in made:
            mail.recv(i)
        return (slots[0] + slots[1]) + (slots[2] + slots[3])

    t2[...] = stage(t1, xin, x, xs)
    full = stage(t2, yin, y, ys)
    t3[...] = full[0:32]
    v_out[pl.ds(32, 16)] = full[32:48]
    v_out[pl.ds(0, 32)] = stage(t3, zin, z, zs)
    for i in ps:
        mail.recv(i)
    own.wait()
    mail.close()


def finish(p, v):
    return comm_call(
        finish_kernel, "finish", 6, 16,
        [((4, 96, 768), BF), ((48, 128), F32)],
        [
            pltpu.VMEM((48, 128), F32),
            pltpu.VMEM((4, 48, 128), F32),
            pltpu.VMEM((4, 48, 128), F32),
            pltpu.VMEM((4, 32, 128), F32),
            pltpu.VMEM((48, 128), F32),
            pltpu.VMEM((48, 128), F32),
            pltpu.VMEM((32, 128), F32),
        ],
        [p, v],
        [False, True],
        [False, True],
    )


NT = (((1,), (1,)), ((), ()))


def attention_forward_kernel(a_ref, kv_ref, kpos_ref, qpos_ref, o_ref, st_ref, kvt):
    lane = lax.broadcasted_iota(jnp.int32, (384, 128), 1)
    for h in range(3):
        cols = slice(128 * h, 128 * h + 128)
        kvt[...] = kv_ref[:, cols].T

        def tile(j, _):
            a = a_ref[j, :, cols]
            aq = jnp.where(lane < 64, a, jnp.zeros_like(a))
            s = lax.dot_general(kv_ref[:, cols], aq, NT, preferred_element_type=F32)
            kp = kpos_ref[...]
            ok = jnp.concatenate([kp, kp, kp], axis=1) <= qpos_ref[j]
            s = jnp.where(ok, s, -1e30)
            top = jnp.max(s, axis=0, keepdims=True)
            p = jnp.exp(s - top)
            total = jnp.sum(p, axis=0, keepdims=True)
            o = jnp.dot(kvt[...], p.astype(BF), preferred_element_type=F32)[64:128]
            o = o / total
            gt = a.astype(F32).T[64:128]
            o_ref[j, 64 * h : 64 * h + 64, :] = o.astype(BF)
            st_ref[j, h : h + 1, :] = top + jnp.log(total)
            st_ref[j, 4 + h : 5 + h, :] = jnp.sum(o * gt, axis=0, keepdims=True)
            return 0

        lax.fori_loop(0, 4, tile, 0)
    st_ref[:, 3:4, :] = jnp.zeros((4, 1, 384), F32)
    st_ref[:, 7:8, :] = jnp.zeros((4, 1, 384), F32)


def attention_backward_kernel(
    a_ref, kv_ref, kpos_ref, qpos_ref, st_ref, dq_ref, dkv_ref, kvt, acc_k, acc_v
):
    lane = lax.broadcasted_iota(jnp.int32, (384, 128), 1)
    wide = lax.broadcasted_iota(jnp.int32, (1536, 128), 1)
    for h in range(3):
        cols = slice(128 * h, 128 * h + 128)
        kvt[...] = kv_ref[:, cols].T
        acc_k[...] = jnp.zeros_like(acc_k)
        acc_v[...] = jnp.zeros_like(acc_v)

        def tile(j, _):
            a = a_ref[j, :, cols]
            zero = jnp.zeros_like(a)
            aq = jnp.where(lane < 64, a, zero)
            ag = jnp.where(lane < 64, zero, a)
            kv = kv_ref[:, cols]
            s = lax.dot_general(kv, aq, NT, preferred_element_type=F32)
            kp = kpos_ref[...]
            ok = jnp.concatenate([kp, kp, kp], axis=1) <= qpos_ref[j]
            p = jnp.where(ok, jnp.exp(s - st_ref[j, h : h + 1, :]), 0.0)
            gp = lax.dot_general(kv, ag, NT, preferred_element_type=F32)
            gs = (p * (gp - st_ref[j, 4 + h : 5 + h, :])).astype(BF)
            acc_v[...] += jnp.dot(p.astype(BF), a, preferred_element_type=F32)
            acc_k[...] += jnp.dot(gs, a, preferred_element_type=F32)
            dq = jnp.dot(kvt[...], gs, preferred_element_type=F32)[0:64]
            dq_ref[j, 64 * h : 64 * h + 64, :] = (dq * 0.125).astype(BF)
            return 0

        lax.fori_loop(0, 4, tile, 0)
        dkv_ref[:, cols] = jnp.where(wide < 64, acc_k[...], acc_v[...]).astype(BF)


def local_call(kernel, name, outs, scratch, args):
    vspec = pl.BlockSpec(memory_space=pltpu.VMEM)
    return pl.pallas_call(
        kernel,
        name=name,
        out_shape=[jax.ShapeDtypeStruct(*o) for o in outs],
        in_specs=[vspec] * len(args),
        out_specs=[vspec] * len(outs),
        scratch_shapes=scratch,
        compiler_params=pltpu.CompilerParams(vmem_limit_bytes=60 * 1024 * 1024),
    )(*args)


def gelu_parts(pre_act):
    cdf_val = 0.5 * (1.0 + jax.scipy.special.erf(pre_act * 0.7071067811865476))
    pdf_val = jnp.exp(-0.5 * pre_act * pre_act) * 0.3989422804014327
    return cdf_val + pre_act * pdf_val


def dot(spec, a, b):
    return jnp.einsum(spec, a, b, preferred_element_type=F32)


def rotate(t, cosine, sine):
    half = ROT // 2
    first, second = t[..., :half], t[..., half:ROT]
    cb, sb = cosine[:, None, :], sine[:, None, :]
    return jnp.concatenate(
        [first * cb - second * sb, second * cb + first * sb, t[..., ROT:]], axis=-1
    )


def shards(
    layer_input_residual, positions, ln1_gain, ln1_bias, ln2_gain, ln2_bias, w_qkv,
    query_key_value_bias, w_out, b_out, w_up, up_bias_vector, w_down, b_down, grad_out,
):
    c = lax.axis_index("context")
    z = lax.axis_index("tensor")
    x_in = layer_input_residual[0]
    g_in = grad_out[0]
    vec = jnp.stack([ln1_gain, ln1_bias, ln2_gain, ln2_bias, b_out, b_down], axis=1)
    src = jnp.concatenate(
        [w_up, w_down, w_qkv.reshape(24, 576), w_out, jnp.pad(vec, ((0, 0), (0, 122)))], axis=1
    )
    whole = gather_weights(src).reshape(768, WCOLS)
    up_w, down_w = whole[:, :768], whole[:, 768:1536]
    qkv_w, out_w = whole[:, 1536:2112], whole[:, 2112:2304]
    vec_f = whole[:, 2304:2310].astype(F32)
    gain1, bias1, gain2, bias2 = vec_f[:, 0], vec_f[:, 1], vec_f[:, 2], vec_f[:, 3]
    bias_sum = vec_f[:, 4] + vec_f[:, 5]

    centered = x_in - jnp.mean(x_in, axis=-1, keepdims=True)
    rstd = lax.rsqrt(jnp.mean(centered * centered, axis=-1, keepdims=True) + norm_eps)
    xhat = centered * rstd
    n1 = (xhat * gain1 + bias1).astype(BF)
    n2 = (xhat * gain2 + bias2).astype(BF)
    gbf = g_in.astype(BF)

    proj = dot("td,dj->tj", n1, qkv_w) + query_key_value_bias.reshape(1, 576)
    pos16 = positions.reshape(4, 4, 384)
    own_pos = lax.dynamic_slice_in_dim(positions.reshape(16, 384), c, 1, 0)[0]
    freqs = jnp.exp(-(jnp.arange(8).astype(F32) * (2.0 / ROT)) * math.log(10000.0))
    angles = own_pos.astype(F32)[:, None] * freqs
    cosine, sine = jnp.cos(angles), jnp.sin(angles)
    q = rotate(proj[:, :192].reshape(384, 3, HS), cosine, sine).astype(BF) * BF(0.125)
    kk = rotate(proj[:, 192:384].reshape(384, 3, HS), cosine, sine).astype(BF)
    vv = proj[:, 384:].reshape(384, 3, HS).astype(BF)
    ga = dot("td,di->ti", gbf, out_w).astype(BF).reshape(384, 3, HS)
    a_own = jnp.concatenate([q, ga], axis=-1).reshape(384, 384)
    kv_own = jnp.concatenate([kk, vv], axis=-1).reshape(384, 384)

    pre_act = dot("td,df->tf", n2, up_w) + up_bias_vector
    act = jax.nn.gelu(pre_act, approximate=False).astype(BF)
    g_pre = dot("td,df->tf", gbf, down_w) * gelu_parts(pre_act)
    g_b_up = jnp.sum(g_pre, axis=0)
    g_pre_bf = g_pre.astype(BF)
    g_n2 = dot("tf,df->td", g_pre_bf, up_w).astype(BF).reshape(4, 96, 768)

    a_all, kv_all, n2_parts = gather_attention(a_own, kv_own, g_n2)

    qpos = lax.dynamic_slice_in_dim(pos16, lax.rem(c, 4), 1, 1)
    kpos = lax.dynamic_slice_in_dim(pos16, lax.div(c, 4), 1, 0).reshape(1536, 1)
    kpos = jnp.broadcast_to(kpos, (1536, 128))
    kv_flat = kv_all.reshape(1536, 384)
    o_part, st_part = local_call(
        attention_forward_kernel, "attention_forward",
        [((4, 192, 384), BF), ((4, 8, 384), F32)],
        [pltpu.VMEM((128, 1536), BF)],
        [a_all, kv_flat, kpos, qpos],
    )
    o_all, st_all = share_partials(o_part, st_part.transpose(1, 0, 2).reshape(8, 1536))
    lse_i, del_i = st_all[:, 0:4], st_all[:, 4:8]
    top = jnp.max(lse_i, axis=0)
    lse = top + jnp.log(jnp.sum(jnp.exp(lse_i - top), axis=0))
    share = jnp.exp(lse_i - lse)
    delta = jnp.sum(share * del_i, axis=0)
    st = jnp.concatenate([lse, delta], axis=0).reshape(8, 4, 384).transpose(1, 0, 2)
    own_share = lax.dynamic_slice_in_dim(share, lax.div(c, 4) * 384, 384, 2)[:, :3]
    attended = (
        jnp.sum(own_share[:, :, None, :] * o_all.reshape(4, 3, 64, 384).astype(F32), axis=0)
        .astype(BF)
        .reshape(192, 384)
    )
    branch = dot("it,di->td", attended, out_w) + dot("tf,df->td", act, down_w)
    branch = branch.astype(BF).reshape(4, 96, 768)

    dq_part, dkv_part = local_call(
        attention_backward_kernel, "attention_backward",
        [((4, 192, 384), BF), ((1536, 384), BF)],
        [pltpu.VMEM((128, 1536), BF), pltpu.VMEM((1536, 128), F32), pltpu.VMEM((1536, 128), F32)],
        [a_all, kv_flat, kpos, qpos, st],
    )
    dq_all, dkv, br_all = reduce_attention(dq_part, dkv_part.reshape(4, 384, 384), branch)
    layer_out = x_in + br_all.reshape(384, 768).astype(F32) + bias_sum

    dq = jnp.sum(dq_all.astype(F32), axis=0).T.reshape(384, 3, HS)
    dkv = dkv.reshape(384, 3, 2, HS)
    g_q = rotate(dq, cosine, -sine).reshape(384, 192)
    g_k = rotate(dkv[:, :, 0], cosine, -sine).reshape(384, 192)
    g_v = dkv[:, :, 1].reshape(384, 192)
    g_proj = jnp.concatenate([g_q, g_k, g_v], axis=1)
    g_b_qkv = jnp.sum(g_proj, axis=0)
    g_proj_bf = g_proj.astype(BF)
    g_n1 = dot("tj,dj->td", g_proj_bf, qkv_w).astype(BF).reshape(4, 96, 768)

    grads = jnp.concatenate(
        [
            dot("td,tf->df", n2, g_pre_bf).astype(BF),
            dot("td,tf->df", gbf, act).astype(BF),
            dot("td,tj->dj", n1, g_proj_bf).astype(BF),
            dot("td,it->di", gbf, attended).astype(BF),
        ],
        axis=1,
    )
    grads = grads.reshape(2, 4, 2, 2, 24, 2, GHALF)
    along_x = grads[..., 0, :].transpose(3, 1, 2, 0, 4, 5).reshape(2, 4, 4, 24, GHALF)
    along_y = grads[..., 1, :].transpose(3, 2, 0, 1, 4, 5).reshape(2, 4, 4, 24, GHALF)
    own_w, n1_parts = reduce_weights(jnp.stack([along_x, along_y], axis=1), g_n1)
    own_w = jnp.concatenate([own_w[0], own_w[1]], axis=1)

    s1 = jnp.sum(n1_parts.astype(F32), axis=0)
    s2 = jnp.sum(n2_parts.astype(F32), axis=0)
    xh = lax.dynamic_slice_in_dim(xhat, z * 96, 96, 0)
    rs = lax.dynamic_slice_in_dim(rstd, z * 96, 96, 0)
    go = lax.dynamic_slice_in_dim(g_in, z * 96, 96, 0)

    def norm_back(g, gain):
        u = g * gain
        return rs * (
            u
            - jnp.mean(u, axis=-1, keepdims=True)
            - xh * jnp.mean(u * xh, axis=-1, keepdims=True)
        )

    piece = (norm_back(s1, gain1) + norm_back(s2, gain2)).astype(BF)
    sums = jnp.stack(
        [
            jnp.sum(s1 * xh, axis=0), jnp.sum(s1, axis=0),
            jnp.sum(s2 * xh, axis=0), jnp.sum(s2, axis=0), jnp.sum(go, axis=0),
        ]
    )
    small = jnp.concatenate(
        [
            jnp.pad(sums.reshape(30, 128), ((0, 2), (0, 0))),
            jnp.pad(jnp.concatenate([g_b_qkv, g_b_up]), (0, 704)).reshape(16, 128),
        ]
    )
    rows, small = finish(piece, small)
    grad_in = g_in + rows.reshape(384, 768).astype(F32)
    mine = lax.axis_index("shard") * 16 + c
    own_vec = lax.dynamic_slice_in_dim(small[:30].reshape(5, 768), mine * 24, 24, 1)
    biases = small[32:48].reshape(2048)
    return (
        layer_out[None], grad_in[None],
        own_vec[0], own_vec[1], own_vec[2], own_vec[3],
        own_w[:, 1536:2112].reshape(24, 3, 192),
        biases[:576].reshape(3, 192),
        own_w[:, 2112:2304],
        own_vec[4],
        own_w[:, :768],
        biases[576:1344],
        own_w[:, 768:1536],
        own_vec[4],
    )


def solution(mesh):
    rows = P(("shard", "context"))
    token = P("shard", "context", None)
    wide = P(("shard", "context"), "tensor")
    qkv = P(("shard", "context"), None, "tensor")
    in_specs = (
        token, P("shard", None), rows, rows, rows, rows, qkv, P(None, "tensor"),
        wide, rows, wide, P("tensor"), wide, rows, token,
    )
    out_specs = (
        token, token, rows, rows, rows, rows, qkv, P(None, "tensor"),
        wide, rows, wide, P("tensor"), wide, rows,
    )
    return jax.shard_map(shards, mesh=mesh, in_specs=in_specs, out_specs=out_specs, check_vma=False)
```

time: 1270 us -> 261 us (0.21)
  waiting for transfers between devices: 705 us -> 0 us
  blocking collectives: 245 us -> 0 us
  Pallas kernels: 0 us -> 171 us
  matrix products: 183 us -> 23.5 us
  local copies, waits for them, and re-layouts: 73.6 us -> 39.7 us
  between operations: 15.5 us -> 1.3 us
    reduce_scatter x4 -> x0, waiting for transfers between devices: 425 us -> none  [the longest x1 138 us: shards(): lax.psum_scatter(query_key_value_weight_gradient, ('shard', 'context'), s...]
    unnamed x14 -> x0, waiting for transfers between devices: 179 us -> none
    pallas_call x0 -> x8, Pallas kernels: none -> 171 us  [the longest x6 127 us: comm_call(): pl.pallas_call(kernel, name=name, out_shape=[jax.ShapeDtypeStruct(*o) for...]
    dot_general x96 -> x12, matrix products: 183 us -> 23.5 us  [dot(): return jnp.einsum(spec, a, b, preferred_element_type=F32)]
    unnamed x1 -> x0, blocking collectives: 123 us -> none
    all_gather x3 -> x0, blocking collectives: 121 us -> none  [the longest x1 41.9 us: shards(): lax.all_gather(vec_local, ('shard', 'context'), axis=0, tiled=True)]
    all_gather x4 -> x0, waiting for transfers between devices: 58.1 us -> none  [the longest x1 51.8 us: shards(): val_piece = lax.all_gather(values_flat, 'context', axis=1, tiled=True)]
    dynamic_slice x48 -> x3, local copies, waits for them, and re-layouts: 49.9 us -> 0.68 us  [the longest x1 0.61 us: shards(): qpos = lax.dynamic_slice_in_dim(pos16, lax.rem(c, 4), 1, 1)]
  transfers between devices with their start and end apart: 12 -> 0, of which waited for: 9 -> 0; matrix products, arithmetic and copies ran while one was open for 22% -> 0% of each run, Pallas kernels for 0% -> 0%
where the time goes in v1:
time: 261 us; the launch traced here: 260 us
  Pallas kernels  171 us (66%)
  local copies, waits for them, and re-layouts  39.7 us (15%)
  other arithmetic  24.8 us (10%)
  matrix products  23.5 us (9%)
    pallas_call x6, Pallas kernels, comm_call(): pl.pallas_call(kernel, name=name, out_shape=[jax.ShapeDtypeStruct(*o) for...  127 us
    pallas_call x2, Pallas kernels, local_call(): pl.pallas_call(kernel, name=name, out_shape=[jax.ShapeDtypeStruct(*o) for...  44.2 us
    dot_general x12, matrix products, dot(): return jnp.einsum(spec, a, b, preferred_element_type=F32)  23.5 us
    slice x1, local copies, waits for them, and re-layouts, shards(): grads[..., 0, :].transpose(3, 1, 2, 0, 4, 5).reshape(2, 4, 4, 24, GHALF)  9.43 us
    reshape x1, local copies, waits for them, and re-layouts, shards(): grads = grads.reshape(2, 4, 2, 2, 24, 2, GHALF)  6.84 us

profile of v1, /device:TPU:1, one launch (start us, length us, event | category | flops | bytes accessed | tf_op | source)
XLA Modules:
  0.0 260.3 jit_solution(14933820796080163957)
XLA Ops:
  0.7 0.9 stack.48
  1.6 1.5 reduce_sum.171
  5.4 0.7 reduce.22
  6.8 0.7 fusion.42
  7.6 0.7 concatenate.43.src
  8.4 1.1 broadcast_in_dim.5.kpos_ref
  9.8 24.7 %gather_weights.1 = bf16[32,24,2432]{2,1,0:T(8,128)(2,1)} custom-call(bf16[24,2432]{1,0:T(8,128)(2,1)} %concatenate.43.src), custom_call_target="tpu_custom_call" | custom-call | tf_op jit(solution)/shard_map/gather_weights/pallas_call | solution.py:76
  34.5 1.7 convolution_convert_fusion.6
  36.2 0.9 slice.196
  37.9 1.9 convolution_add_fusion.2
  40.6 0.9 copy.81.kv_ref
  41.5 0.8 maximum_multiply_fusion
  42.3 0.9 copy.80.a_ref
  43.2 4.6 %fusion.9 = (bf16[384,768]{1,0:T(8,128)(2,1)S(1)}, f32[384,768]{1,0:T(8,128)S(1)}) fusion(f32[768]{0:T(1024)} %param.26, bf16[768,2432]{1,0:T(8,128)(2,1)} %bitcast.113, f32[384,768]{1,0:T(8,128)S(1)} %fusion.20, f32[768]{0:T(1024)} %get-tuple-element.115, f32[768]{0:T(1024)S(1)} %get-tuple-element.116), kind=kOutput, calls=%fused_computation.27 | convolution fusion | flops 473333760 | bytes 4140032 | tf_op jit(solution)/shard_map/td,df->tf/dot_general | solution.py:630
  47.8 1.4 fusion.49
  49.2 1.5 convolution_convert_fusion.4
  50.7 1.9 convolution_convert_fusion.1
  52.6 1.8 fusion.1
  54.4 27.5 %gather_attention.1 = (bf16[4,384,384]{2,1,0:T(8,128)(2,1)}, bf16[4,384,384]{2,1,0:T(8,128)(2,1)}, bf16[4,96,768]{2,1,0:T(8,128)(2,1)}) custom-call(bf16[384,384]{1,0:T(8,128)(2,1)} %copy.80.a_ref, bf16[384,384]{1,0:T(8,128)(2,1)} %copy.81.kv_ref, bf16[4,96,768]{2,1,0:T(8,128)(2,1)} %bitcast.144), custom_call_target="tpu_custom_call" | custom-call | tf_op jit(solution)/shard_map/gather_attention/pallas_call | solution.py:76
  82.0 2.0 convert_reduce_fusion
  84.6 18.2 %attention_forward.1 = (bf16[4,192,384]{2,1,0:T(8,128)(2,1)}, f32[4,8,384]{2,1,0:T(8,128)}) custom-call(bf16[4,384,384]{2,1,0:T(8,128)(2,1)} %get-tuple-element.30.a_ref, bf16[1536,384]{1,0:T(8,128)(2,1)} %bitcast.121, s32[1536,128]{1,0:T(8,128)} %broadcast_in_dim.5.kpos_ref, s32[4,1,384]{2,1,0:T(1,128)} %constant_dynamic-slice_fusion.2.qpos_ref), custom_call_target="tpu_custom_call" | custom-call | tf_op jit(solution)/shard_map/attention_forward/pallas_call | solution.py:612
  102.8 12.5 %share_partials.1 = (bf16[4,192,384]{2,1,0:T(8,128)(2,1)}, f32[4,8,1536]{2,1,0:T(8,128)}) custom-call(bf16[4,192,384]{2,1,0:T(8,128)(2,1)} %get-tuple-element.32.o_ref, f32[8,1536]{1,0:T(8,128)} %bitcast.152), custom_call_target="tpu_custom_call" | custom-call | tf_op jit(solution)/shard_map/share_partials/pallas_call | solution.py:76
  115.3 1.0 slice_reduce_fusion
  116.2 1.0 exponential_reduce_fusion
  117.3 1.1 multiply_reduce_fusion.7
  119.0 26.0 %attention_backward.1 = (bf16[4,192,384]{2,1,0:T(8,128)(2,1)}, bf16[1536,384]{1,0:T(8,128)(2,1)}) custom-call(bf16[4,384,384]{2,1,0:T(8,128)(2,1)} %get-tuple-element.30.a_ref, bf16[1536,384]{1,0:T(8,128)(2,1)} %bitcast.122, s32[1536,128]{1,0:T(8,128)} %broadcast_in_dim.5.kpos_ref, s32[4,1,384]{2,1,0:T(1,128)} %constant_dynamic-slice_fusion.2.qpos_ref, ...), custom_call_target="tpu_custom_call" | custom-call | tf_op jit(solution)/shard_map/attention_backward/pallas_call | solution.py:612
  145.0 1.2 fusion.11
  146.2 1.0 fusion.19
  147.2 1.6 fusion.33
  148.8 2.8 %fusion.2 = bf16[384,768]{1,0:T(8,128)(2,1)} fusion(f32[384,768]{1,0:T(8,128)S(1)} %fusion.33, bf16[384,768]{1,0:T(8,128)(2,1)S(1)} %get-tuple-element.151, bf16[768,2432]{1,0:T(8,128)(2,1)} %bitcast.115), kind=kOutput, calls=%fused_computation.17 | convolution fusion | flops 453574656 | bytes 3538944 | tf_op jit(solution)/shard_map/tf,df->td/dot_general | solution.py:630
  151.6 19.4 %reduce_attention.1 = (bf16[4,192,384]{2,1,0:T(8,128)(2,1)}, f32[384,384]{1,0:T(8,128)}, bf16[4,96,768]{2,1,0:T(8,128)(2,1)}) custom-call(bf16[4,192,384]{2,1,0:T(8,128)(2,1)} %get-tuple-element.35.dq_ref, bf16[4,384,384]{2,1,0:T(8,128)(2,1)} %bitcast.136, bf16[4,96,768]{2,1,0:T(8,128)(2,1)} %bitcast.132), custom_call_target="tpu_custom_call" | custom-call | tf_op jit(solution)/shard_map/reduce_attention/pallas_call | solution.py:76
  171.0 1.2 convert_reduce_fusion.4
  172.3 1.1 fusion.10
  174.3 2.7 %convolution_convert_fusion.3 = bf16[384,768]{1,0:T(8,128)(2,1)} fusion(bf16[768,2432]{1,0:T(8,128)(2,1)} %bitcast.116, f32[384,192]{0,1:T(8,128)S(1)} %bitcast.123, f32[384,192]{0,1:T(8,128)S(1)} %bitcast.129, f32[384,192]{0,1:T(8,128)S(1)} %bitcast.126), kind=kOutput, calls=%fused_computation.18 | convolution fusion | flops 341360640 | bytes 2457600 | tf_op jit(solution)/shard_map/tj,dj->td/dot_general | solution.py:630
  177.0 0.8 fusion.27
  179.8 3.9 %copy.83 = bf16[768,2304]{1,0:T(8,128)(2,1)} copy(bf16[768,2304]{0,1:T(8,128)(2,1)S(1)} %pad_maximum_fusion) | data formatting | bytes 7077888 | tf_op jit(solution)/shard_map/concatenate | solution.py:735
  183.8 6.8 %reshape.329 = bf16[2,4,2,2,24,2,1152]{6,5,4,3,2,1,0:T(2,128)(2,1)S(1)} reshape(bf16[768,2304]{1,0:T(8,128)(2,1)} %copy.83) | data formatting | bytes 7077888 | tf_op jit(solution)/shard_map/reshape | solution.py:744
  190.6 0.8 fusion.40
  191.4 9.4 %fusion.47 = (bf16[2,4,2,2,24,1,1152]{6,5,4,3,2,1,0:T(2,128)(2,1)}, bf16[2,4,2,2,24,1,1152]{6,5,4,3,2,1,0:T(2,128)(2,1)}) fusion(bf16[2,4,2,2,24,2,1152]{6,5,4,3,2,1,0:T(2,128)(2,1)S(1)} %reshape.329), kind=kLoop, calls=%fused_computation.144 | loop fusion | bytes 7077888 | tf_op jit(solution)/shard_map/slice | solution.py:745
  200.8 2.4 copy.90
  204.2 2.2 pad_maximum_fusion.1.g_ref
  206.3 26.1 %reduce_weights.1 = (f32[2,24,1152]{2,1,0:T(8,128)}, bf16[4,96,768]{2,1,0:T(8,128)(2,1)}) custom-call(bf16[2,2,4,4,24,1152]{5,4,3,2,1,0:T(8,128)(2,1)} %pad_maximum_fusion.1.g_ref, bf16[4,96,768]{2,1,0:T(8,128)(2,1)} %bitcast.146), custom_call_target="tpu_custom_call" | custom-call | tf_op jit(solution)/shard_map/reduce_weights/pallas_call | solution.py:76
  232.5 1.3 convert_reduce_fusion.2
  234.1 0.8 multiply_convert_fusion.p_ref
  237.8 16.5 %finish.1 = (bf16[4,96,768]{2,1,0:T(8,128)(2,1)}, f32[48,128]{1,0:T(8,128)}) custom-call(bf16[96,768]{1,0:T(8,128)(2,1)} %multiply_convert_fusion.p_ref, f32[48,128]{1,0:T(8,128)} %select_maximum_fusion.v_ref), custom_call_target="tpu_custom_call" | custom-call | tf_op jit(solution)/shard_map/finish/pallas_call | solution.py:76
  254.2 0.7 slice_bitcast_fusion.3
  254.9 0.7 slice.181
  257.6 2.2 convert_add_fusion
  (130 shorter events, 15.3 us)
Async XLA Ops:
  0.6 2.5 copy-start
  1.5 2.6 copy-start.28
  1.6 2.7 %copy-start.5 = (f32[1,384,768]{2,1,0:T(8,128)S(1)}, f32[1,384,768]{2,1,0:T(8,128)}, u32[]{:S(2)}) copy-start(f32[1,384,768]{2,1,0:T(8,128)} %param.29) | copy-start | bytes 3538948
  1.6 3.8 %copy-start.14 = (s32[1,6144]{1,0:T(1,128)S(1)}, s32[1,6144]{1,0:T(1,128)}, u32[]{:S(2)}) copy-start(s32[1,6144]{1,0:T(1,128)} %param.16) | copy-start | bytes 73732
  3.1 4.4 %copy-start.18 = (bf16[24,3,192]{2,0,1:T(8,128)(2,1)S(1)}, bf16[24,3,192]{2,0,1:T(8,128)(2,1)}, u32[]{:S(2)}) copy-start(bf16[24,3,192]{2,0,1:T(8,128)(2,1)} %param.21) | copy-start | bytes 82948
  3.1 4.5 %copy-start.19 = (bf16[24,768]{1,0:T(8,128)(2,1)S(1)}, bf16[24,768]{1,0:T(8,128)(2,1)}, u32[]{:S(2)}) copy-start(bf16[24,768]{1,0:T(8,128)(2,1)} %param.25) | copy-start | bytes 110596
  3.1 4.5 %copy-start.20 = (bf16[24,768]{1,0:T(8,128)(2,1)S(1)}, bf16[24,768]{1,0:T(8,128)(2,1)}, u32[]{:S(2)}) copy-start(bf16[24,768]{1,0:T(8,128)(2,1)} %param.27) | copy-start | bytes 110596
  3.1 4.5 %copy-start.27 = (bf16[24,192]{1,0:T(8,128)(2,1)S(1)}, bf16[24,192]{1,0:T(8,128)(2,1)}, u32[]{:S(2)}) copy-start(bf16[24,192]{1,0:T(8,128)(2,1)} %param.23) | copy-start | bytes 27652
  9.8 168.0 %copy-start.1 = (f32[384,768]{1,0:T(8,128)}, f32[384,768]{1,0:T(8,128)S(1)}, u32[]{:S(2)}) copy-start(f32[384,768]{1,0:T(8,128)S(1)} %fusion.20) | copy-start | bytes 3538948
  37.9 1.9 copy-start.15
  37.9 1.9 copy-start.21
  43.2 4.6 %copy-start.4 = (bf16[32,24,2432]{2,1,0:T(8,128)(2,1)S(1)}, bf16[32,24,2432]{2,1,0:T(8,128)(2,1)}, u32[]{:S(2)}) copy-start(bf16[32,24,2432]{2,1,0:T(8,128)(2,1)} %gather_weights.1) | copy-start | bytes 11206660
  49.2 1.5 copy-start.24
  171.0 1.3 copy-start.12
  171.0 1.3 copy-start.23
  172.3 1.1 copy-start.11
  173.5 0.7 copy-start.17
  174.3 3.5 %copy-start.16 = (f32[768]{0:T(1024)S(1)}, f32[768]{0:T(1024)}, u32[]{:S(2)}) copy-start(f32[768]{0:T(1024)} %copy-done.15) | copy-start | bytes 9220
  174.3 3.5 %copy-start.22 = (f32[768]{0:T(1024)S(1)}, f32[768]{0:T(1024)}, u32[]{:S(2)}) copy-start(f32[768]{0:T(1024)} %copy-done.21) | copy-start | bytes 9220
  177.8 1.3 copy-start.7
  177.8 1.6 copy-start.9
  177.8 1.7 copy-start.10
  200.8 3.1 %copy-start.3 = (bf16[2,4,2,2,24,1,1152]{6,5,4,3,2,1,0:T(2,128)(2,1)S(1)}, bf16[2,4,2,2,24,1,1152]{6,5,4,3,2,1,0:T(2,128)(2,1)}, u32[]{:S(2)}) copy-start(bf16[2,4,2,2,24,1,1152]{6,5,4,3,2,1,0:T(2,128)(2,1)} %get-tuple-element.122) | copy-start | bytes 5308420
  206.3 27.5 %copy-start.2 = (f32[384,768]{1,0:T(8,128)S(1)}, f32[384,768]{1,0:T(8,128)}, u32[]{:S(2)}) copy-start(f32[384,768]{1,0:T(8,128)} %copy-done.1) | copy-start | bytes 3538948
  206.3 27.5 %copy-start.8 = (f32[96,768]{1,0:T(8,128)S(1)}, f32[96,768]{1,0:T(8,128)}, u32[]{:S(2)}) copy-start(f32[96,768]{1,0:T(8,128)} %get-tuple-element.109) | copy-start | bytes 884740
  232.5 1.7 copy-start.29
  233.8 1.2 copy-start.25
  233.8 1.2 copy-start.26
  233.8 1.8 copy-start.13
  235.0 22.6 %copy-start.6 = (f32[1,384,768]{2,1,0:T(8,128)S(1)}, f32[1,384,768]{2,1,0:T(8,128)}, u32[]{:S(2)}) copy-start(f32[1,384,768]{2,1,0:T(8,128)} %param.29) | copy-start | bytes 3538948
  257.6 2.2 copy-start.30

commit v2 on v1

v2 whole, which is shorter than its diff:
```python
import functools
import math

import jax
import jax.numpy as jnp
from jax import lax
from jax.experimental import pallas as pl
from jax.experimental.pallas import tpu as pltpu
from jax.sharding import PartitionSpec as P

HS = 64
ROT = 16
BF = jnp.bfloat16
F32 = jnp.float32
MESH = pl.DeviceIdType.MESH
norm_eps = 1e-05


def coords():
    s = lax.axis_index("shard")
    c = lax.axis_index("context")
    z = lax.axis_index("tensor")
    x = lax.div(c, 4)
    yh = lax.rem(lax.div(c, 2), 2)
    k = lax.rem(c, 2)
    return x, yh * 2 + s, k, z


def dev(x, y, k, z):
    return (lax.rem(y, 2), x * 4 + lax.div(y, 2) * 2 + k, z)


def m4(a):
    return lax.rem(a, 4)


class Mail:
    def __init__(self, send_sems, recv_sems):
        self.send_sems, self.recv_sems, self.made = send_sems, recv_sems, []

    def send(self, src, dst, device):
        i = len(self.made)
        assert i < self.send_sems.shape[0]
        copy = pltpu.make_async_remote_copy(
            src_ref=src,
            dst_ref=dst,
            send_sem=self.send_sems.at[i],
            recv_sem=self.recv_sems.at[i],
            device_id=device,
            device_id_type=MESH,
        )
        copy.start()
        self.made.append(copy)
        return i

    def recv(self, i):
        self.made[i].wait_recv()

    def close(self):
        for copy in self.made:
            copy.wait_send()


def greet(devices):
    barrier = pltpu.get_barrier_semaphore()
    for device in devices:
        pl.semaphore_signal(barrier, inc=1, device_id=device, device_id_type=MESH)
    pl.semaphore_wait(barrier, len(devices))


class Bounce:
    def __init__(self, src, via, dst, sem_in, sem_out):
        self.first = pltpu.make_async_copy(src, via, sem_in)
        self.last = pltpu.make_async_copy(via, dst, sem_out)
        self.first.start()

    def turn(self):
        self.first.wait()
        self.last.start()

    def wait(self):
        self.last.wait()


def comm_call(kernel, name, cid, n_copies, outs, scratch, args, in_vmem=None, out_vmem=None):
    anyspec = pl.BlockSpec(memory_space=pl.ANY)
    vspec = pl.BlockSpec(memory_space=pltpu.VMEM)
    in_vmem = in_vmem or [False] * len(args)
    out_vmem = out_vmem or [False] * len(outs)
    return pl.pallas_call(
        kernel,
        name=name,
        out_shape=[jax.ShapeDtypeStruct(*o) for o in outs],
        in_specs=[vspec if v else anyspec for v in in_vmem],
        out_specs=[vspec if v else anyspec for v in out_vmem],
        scratch_shapes=list(scratch)
        + [
            pltpu.SemaphoreType.DMA((n_copies,)),
            pltpu.SemaphoreType.DMA((n_copies,)),
            pltpu.SemaphoreType.DMA((6,)),
        ],
        compiler_params=pltpu.CompilerParams(
            collective_id=cid, has_side_effects=True, vmem_limit_bytes=56 * 1024 * 1024
        ),
    )(*args)


WCOLS = 2432
P_CUT = (0, 640, 1280)
Q_CUT = (1280, 1792, 2432)


def gather_weights_kernel(src, out, via, ss, rs, ls):
    x, y, k, z = coords()
    mail = Mail(ss, rs)

    def row(xx, yy):
        return lax.rem(yy, 2) * 16 + xx * 4 + lax.div(yy, 2) * 2 + k

    xs = [x, m4(x + 3), m4(x + 1), m4(x + 2)]
    ys = [y, m4(y + 3), m4(y + 1), m4(y + 2)]
    mate = dev(x, y, 1 - k, z)
    step = {
        "x": (dev(xs[2], y, k, z), dev(xs[1], y, k, z)),
        "y": (dev(x, ys[2], k, z), dev(x, ys[1], k, z)),
    }
    greet([step["x"][0], step["x"][1], step["y"][0], step["y"][1], mate])
    me = row(x, y)
    own = Bounce(src, via, out.at[me], ls.at[0], ls.at[1])

    def part(r, lo, hi):
        return out.at[r, :, pl.ds(lo, hi - lo)]

    def begin(view, r, cut, axis):
        return [
            mail.send(view, part(r, cut[0], cut[2]), step[axis][0]),
            mail.send(view, part(r, cut[0], cut[2]), step[axis][1]),
        ]

    def own_view(cut):
        return src.at[:, pl.ds(cut[0], cut[2] - cut[0])]

    mates = []

    def to_mate(r, lo, hi):
        mates.append(mail.send(part(r, lo, hi), part(r, lo, hi), mate))

    plans = [("x", "y", P_CUT), ("y", "x", Q_CUT)]
    first = [begin(own_view(cut), me, cut, a) for a, b, cut in plans]
    second = [[begin(own_view(cut), me, cut, b)] for a, b, cut in plans]
    mates.append(mail.send(src, out.at[me], mate))

    def at(a, i, j):
        return row(xs[i], ys[j]) if a == "x" else row(xs[j], ys[i])

    own.turn()
    relays = [[], []]
    for i in (1, 2):
        for n, (a, b, cut) in enumerate(plans):
            mail.recv(first[n][i - 1])
            r = at(a, i, 0)
            lo, hi = (cut[0], cut[1]) if i == 1 else (cut[1], cut[2])
            relays[n].append(mail.send(part(r, lo, hi), part(r, lo, hi), step[a][i - 1]))
            second[n].append(begin(part(r, cut[0], cut[2]), r, cut, b))
            to_mate(r, cut[0], cut[2])
    for n, (a, b, cut) in enumerate(plans):
        for i in relays[n]:
            mail.recv(i)
        r = at(a, 3, 0)
        second[n].append(begin(part(r, cut[0], cut[2]), r, cut, b))
        to_mate(r, cut[0], cut[2])
    late = []
    for i in range(4):
        for n, (a, b, cut) in enumerate(plans):
            pair = []
            for j in (1, 2):
                mail.recv(second[n][i][j - 1])
                r = at(a, i, j)
                lo, hi = (cut[0], cut[1]) if j == 1 else (cut[1], cut[2])
                pair.append(mail.send(part(r, lo, hi), part(r, lo, hi), step[b][j - 1]))
                to_mate(r, cut[0], cut[2])
            late.append((pair, at(a, i, 3), cut))
    for pair, r, cut in late:
        for i in pair:
            mail.recv(i)
        to_mate(r, cut[0], cut[2])
    for i in mates:
        mail.recv(i)
    own.wait()
    mail.close()


def gather_weights(src):
    return comm_call(
        gather_weights_kernel, "gather_weights", 1, 80,
        [((32, 24, WCOLS), BF)], [pltpu.VMEM((24, WCOLS), BF)], [src],
    )[0]


def spread_z(mail, z, x, y, k, src, dst):
    made = []
    for d in (1, 3, 2):
        peer = m4(z + d)
        made.append(mail.send(src.at[peer], dst.at[z], dev(x, y, k, peer)))
    return made


def gather_attention_kernel(a_ref, kv_ref, n2_ref, a_out, kv_out, n2_out, relay, via_a, via_kv, via_n, ss, rs, ls):
    x, y, k, z = coords()
    mail = Mail(ss, rs)
    xl, xr = m4(x + 3), m4(x + 1)
    right, left = dev(xr, y, k, z), dev(xl, y, k, z)
    up, down = dev(x, m4(y + 1), k, z), dev(x, m4(y + 3), k, z)
    mate = dev(x, y, 1 - k, z)
    greet([right, left, up, down, mate] + [dev(x, y, k, m4(z + d)) for d in (1, 2, 3)])
    slot = lax.div(y, 2) * 2 + k
    far = (1 - lax.div(y, 2)) * 2 + k
    top, low = pl.ds(0, 192), pl.ds(192, 192)
    y1 = mail.send(kv_ref.at[top], relay.at[0], up)
    y2 = mail.send(kv_ref.at[low], relay.at[1], down)
    x1 = mail.send(a_ref, a_out.at[x], right)
    x2 = mail.send(a_ref, a_out.at[x], left)
    c1 = mail.send(kv_ref, kv_out.at[slot], mate)
    zs = spread_z(mail, z, x, y, k, n2_ref, n2_out)
    locals_ = [
        Bounce(a_ref, via_a, a_out.at[x], ls.at[0], ls.at[1]),
        Bounce(kv_ref, via_kv, kv_out.at[slot], ls.at[2], ls.at[3]),
        Bounce(n2_ref.at[z], via_n, n2_out.at[z], ls.at[4], ls.at[5]),
    ]
    for copy in locals_:
        copy.turn()
    up_slot = lax.div(m4(y + 3), 2) * 2 + k
    down_slot = lax.div(m4(y + 1), 2) * 2 + k
    mail.recv(y1)
    y3 = mail.send(relay.at[0], kv_out.at[up_slot, top], up)
    mail.recv(y2)
    y4 = mail.send(relay.at[1], kv_out.at[down_slot, low], down)
    mail.recv(x1)
    x3 = mail.send(a_out.at[xl, top], a_out.at[xl, top], right)
    mail.recv(x2)
    x4 = mail.send(a_out.at[xr, low], a_out.at[xr, low], left)
    mail.recv(y3)
    mail.recv(y4)
    c2 = mail.send(kv_out.at[far], kv_out.at[far], mate)
    for i in [x3, x4, c1, c2] + zs:
        mail.recv(i)
    for copy in locals_:
        copy.wait()
    mail.close()


def gather_attention(a, kv, n2):
    return comm_call(
        gather_attention_kernel, "gather_attention", 2, 16,
        [((4, 384, 384), BF), ((4, 384, 384), BF), ((4, 96, 768), BF)],
        [
            pltpu.VMEM((2, 192, 384), BF),
            pltpu.VMEM((384, 384), BF),
            pltpu.VMEM((384, 384), BF),
            pltpu.VMEM((96, 768), BF),
        ],
        [a, kv, n2],
    )


def exchange_x(mail, x, y, k, z, src, dst, relay):
    xl, xr, xo = m4(x + 3), m4(x + 1), m4(x + 2)
    right, left = dev(xr, y, k, z), dev(xl, y, k, z)
    top, low = pl.ds(0, 96), pl.ds(96, 96)
    r1 = mail.send(src.at[xo, top], relay.at[0], right)
    r2 = mail.send(src.at[xo, low], relay.at[1], left)
    made = [
        mail.send(src.at[xr], dst.at[x], right),
        mail.send(src.at[xl], dst.at[x], left),
    ]

    def finish():
        mail.recv(r1)
        made.append(mail.send(relay.at[0], dst.at[xl, top], right))
        mail.recv(r2)
        made.append(mail.send(relay.at[1], dst.at[xr, low], left))
        return made

    return finish


def share_partials_kernel(o_ref, st_ref, o_out, st_out, relay, via_o, via_st, ss, rs, ls):
    x, y, k, z = coords()
    mail = Mail(ss, rs)
    greet([dev(m4(x + d), y, k, z) for d in (1, 2, 3)])
    made = [mail.send(st_ref, st_out.at[x], dev(m4(x + d), y, k, z)) for d in (1, 3, 2)]
    finish = exchange_x(mail, x, y, k, z, o_ref, o_out, relay)
    own = [
        Bounce(o_ref.at[x], via_o, o_out.at[x], ls.at[0], ls.at[1]),
        Bounce(st_ref, via_st, st_out.at[x], ls.at[2], ls.at[3]),
    ]
    for copy in own:
        copy.turn()
    for i in finish() + made:
        mail.recv(i)
    for copy in own:
        copy.wait()
    mail.close()


def share_partials(o, st):
    return comm_call(
        share_partials_kernel, "share_partials", 3, 12,
        [((4, 192, 384), BF), ((4, 4, 8, 384), F32)],
        [
            pltpu.VMEM((2, 96, 384), BF),
            pltpu.VMEM((192, 384), BF),
            pltpu.VMEM((4, 8, 384), F32),
        ],
        [o, st],
    )


def reduce_attention_kernel(
    dq_ref, dkv_ref, br_ref, dq_out, dkv_out, br_out,
    relay_x, relay_y, mate_in, summed, far_in, z_in, z_sum, via, ss, rs, ls,
):
    x, y, k, z = coords()
    mail = Mail(ss, rs)
    up, down = dev(x, m4(y + 1), k, z), dev(x, m4(y + 3), k, z)
    mate = dev(x, y, 1 - k, z)
    greet(
        [dev(m4(x + 1), y, k, z), dev(m4(x + 3), y, k, z), up, down, mate]
        + [dev(x, y, k, m4(z + d)) for d in (1, 2, 3)]
    )
    yh = lax.div(y, 2)
    far = 1 - yh
    c1 = mail.send(dkv_ref.at[far * 2 + 1 - k], mate_in.at[0], mate)
    c2 = mail.send(dkv_ref.at[yh * 2 + 1 - k], mate_in.at[1], mate)
    zs = spread_z(mail, z, x, y, k, br_ref, z_in)
    finish = exchange_x(mail, x, y, k, z, dq_ref, dq_out, relay_x)
    own = Bounce(dq_ref.at[x], via, dq_out.at[x], ls.at[0], ls.at[2])
    mail.recv(c1)
    summed[...] = (dkv_ref[far * 2 + k].astype(F32) + mate_in[0].astype(F32)).astype(BF)
    top, low = pl.ds(0, 192), pl.ds(192, 192)
    y1 = mail.send(summed.at[top], relay_y.at[0], up)
    y2 = mail.send(summed.at[low], relay_y.at[1], down)
    own.turn()
    mail.recv(c2)
    dkv_out[...] = dkv_ref[yh * 2 + k].astype(F32) + mate_in[1].astype(F32)
    for i in zs:
        mail.recv(i)
    total = br_ref[z].astype(F32)
    for d in (1, 2, 3):
        total = total + z_in[m4(z + d)].astype(F32)
    z_sum[...] = total.astype(BF)
    made = [mail.send(z_sum, br_out.at[z], dev(x, y, k, m4(z + d))) for d in (1, 3, 2)]
    own_z = pltpu.make_async_copy(z_sum, br_out.at[z], ls.at[1])
    own_z.start()
    mail.recv(y1)
    y3 = mail.send(relay_y.at[0], far_in.at[top], up)
    mail.recv(y2)
    y4 = mail.send(relay_y.at[1], far_in.at[low], down)
    made += finish()
    mail.recv(y3)
    mail.recv(y4)
    dkv_out[...] += far_in[...].astype(F32)
    for i in made:
        mail.recv(i)
    own.wait()
    own_z.wait()
    mail.close()


def reduce_attention(dq, dkv, br):
    return comm_call(
        reduce_attention_kernel, "reduce_attention", 4, 24,
        [((4, 192, 384), BF), ((384, 384), F32), ((4, 96, 768), BF)],
        [
            pltpu.VMEM((2, 96, 384), BF),
            pltpu.VMEM((2, 192, 384), BF),
            pltpu.VMEM((2, 384, 384), BF),
            pltpu.VMEM((384, 384), BF),
            pltpu.VMEM((384, 384), BF),
            pltpu.VMEM((4, 96, 768), BF),
            pltpu.VMEM((96, 768), BF),
            pltpu.VMEM((192, 384), BF),
        ],
        [dq, dkv, br],
        [False, True, True],
        [False, True, False],
    )


GCOLS = 2304
GHALF = 1152


def reduce_weights_kernel(
    g_ref, n1_ref, n2_ref, x_ref, rows_ref, v_ref, w_out, p_out, v_out,
    mate_in, e, relay1, fwd1, in1, f, relay2, fwd2, in2,
    n1_in, n1_own, x_own, piece, cin, xin, yin, zin, t1, t2, t3, ss, rs, ls,
):
    x, y, k, z = coords()
    mail = Mail(ss, rs)
    mate = dev(x, y, 1 - k, z)
    step = [
        (dev(m4(x + 1), y, k, z), dev(m4(x + 3), y, k, z)),
        (dev(x, m4(y + 1), k, z), dev(x, m4(y + 3), k, z)),
    ]
    x_peers = [step[0][0], step[0][1], dev(m4(x + 2), y, k, z)]
    y_peers = [step[1][0], step[1][1], dev(x, m4(y + 2), k, z)]
    z_peers = [dev(x, y, k, m4(z + d)) for d in (1, 3, 2)]
    greet([mate] + x_peers + y_peers + z_peers)
    cv = mail.send(v_ref, cin, mate)
    cs = [mail.send(g_ref.at[1 - k, n], mate_in.at[n], mate) for n in range(2)]
    zs = spread_z(mail, z, x, y, k, n1_ref, n1_in)
    own = [
        pltpu.make_async_copy(n1_ref.at[z], n1_own, ls.at[0]),
        pltpu.make_async_copy(x_ref.at[z], x_own, ls.at[1]),
    ]
    for copy in own:
        copy.start()

    def spread(mine, slots, me, peers):
        slots[me] = mine[...]
        return [mail.send(mine, slots.at[me], d) for d in peers]

    def gathered(slots, made):
        for i in made:
            mail.recv(i)
        return (slots[0] + slots[1]) + (slots[2] + slots[3])

    mail.recv(cv)
    t1[...] = v_ref[...] + cin[...]
    vx = spread(t1, xin, x, x_peers)
    pos = (x, y)
    r1 = []
    plain = []
    for n in range(2):
        a = pos[n]
        mail.recv(cs[n])

        def add(i, _):
            e[n, i] = (g_ref[k, n, i].astype(F32) + mate_in[n, i].astype(F32)).astype(BF)
            return 0

        lax.fori_loop(0, 4, add, 0)
        opp = m4(a + 2)
        r1.append(
            (
                mail.send(e.at[n, opp, pl.ds(0, 2)], relay1.at[n, 0], step[n][0]),
                mail.send(e.at[n, opp, pl.ds(2, 2)], relay1.at[n, 1], step[n][1]),
            )
        )
        plain.append(
            (
                mail.send(e.at[n, m4(a + 1), pl.ds(2, 2)], in1.at[n, 0, pl.ds(2, 2)], step[n][0]),
                mail.send(e.at[n, m4(a + 3), pl.ds(0, 2)], in1.at[n, 1, pl.ds(0, 2)], step[n][1]),
            )
        )
    t2[...] = gathered(xin, vx)
    vy = spread(t2, yin, y, y_peers)
    more = []
    for n in range(2):
        a = pos[n]
        mail.recv(r1[n][0])
        fwd1[n, 0] = (
            e[n, m4(a + 1), pl.ds(0, 2)].astype(F32) + relay1[n, 0].astype(F32)
        ).astype(BF)
        m1 = mail.send(fwd1.at[n, 0], in1.at[n, 0, pl.ds(0, 2)], step[n][0])
        mail.recv(r1[n][1])
        fwd1[n, 1] = (
            e[n, m4(a + 3), pl.ds(2, 2)].astype(F32) + relay1[n, 1].astype(F32)
        ).astype(BF)
        m2 = mail.send(fwd1.at[n, 1], in1.at[n, 1, pl.ds(2, 2)], step[n][1])
        more.append((m1, m2))
    for copy in own:
        copy.wait()
    for i in zs:
        mail.recv(i)
    s1 = n1_own[...].astype(F32)
    for d in (1, 2, 3):
        s1 = s1 + n1_in[m4(z + d)].astype(F32)
    s2 = n2_ref[0].astype(F32)
    for d in (1, 2, 3):
        s2 = s2 + n2_ref[d].astype(F32)
    xhat, rstd = standardize(x_own[...])
    back = norm_back(s1 * rows_ref[4:5], xhat, rstd) + norm_back(s2 * rows_ref[5:6], xhat, rstd)
    piece[...] = back.astype(BF)
    ps = [mail.send(piece, p_out.at[z], d) for d in z_peers]
    own_p = pltpu.make_async_copy(piece, p_out.at[z], ls.at[2])
    own_p.start()
    full = gathered(yin, vy)
    t3[...] = full[0:32]
    v_out[pl.ds(32, 16)] = full[32:48]
    vz = spread(t3, zin, z, z_peers)
    r2 = []
    plain2 = []
    c0, c1 = pl.ds(0, 640), pl.ds(640, 512)
    for n in range(2):
        a, b = pos[n], pos[1 - n]
        for i in plain[n] + more[n]:
            mail.recv(i)
        f[n] = (
            e[n, a].astype(F32) + in1[n, 0].astype(F32) + in1[n, 1].astype(F32)
        ).astype(BF)
        go = step[1 - n]
        r2.append(
            (
                mail.send(f.at[n, m4(b + 2), :, c0], relay2.at[n, :, c0], go[0]),
                mail.send(f.at[n, m4(b + 2), :, c1], relay2.at[n, :, c1], go[1]),
            )
        )
        plain2.append(
            (
                mail.send(f.at[n, m4(b + 1), :, c1], in2.at[n, 0, :, c1], go[0]),
                mail.send(f.at[n, m4(b + 3), :, c0], in2.at[n, 1, :, c0], go[1]),
            )
        )
    v_out[pl.ds(0, 32)] = gathered(zin, vz)
    more2 = []
    for n in range(2):
        b = pos[1 - n]
        go = step[1 - n]
        mail.recv(r2[n][0])
        fwd2[n, :, c0] = (
            f[n, m4(b + 1), :, c0].astype(F32) + relay2[n, :, c0].astype(F32)
        ).astype(BF)
        m1 = mail.send(fwd2.at[n, :, c0], in2.at[n, 0, :, c0], go[0])
        mail.recv(r2[n][1])
        fwd2[n, :, c1] = (
            f[n, m4(b + 3), :, c1].astype(F32) + relay2[n, :, c1].astype(F32)
        ).astype(BF)
        m2 = mail.send(fwd2.at[n, :, c1], in2.at[n, 1, :, c1], go[1])
        more2.append((m1, m2))
    for n in range(2):
        b = pos[1 - n]
        for i in plain2[n] + more2[n]:
            mail.recv(i)
        w_out[:, n * GHALF : (n + 1) * GHALF] = (
            f[n, b].astype(F32) + in2[n, 0].astype(F32) + in2[n, 1].astype(F32)
        )
    for i in ps:
        mail.recv(i)
    own_p.wait()
    mail.close()


def reduce_weights(g, n1, n2, x_rows, rows, v):
    def buf(*lead):
        return pltpu.VMEM(lead + (24, GHALF), BF)

    return comm_call(
        reduce_weights_kernel, "reduce_weights", 5, 44,
        [((24, GCOLS), F32), ((4, 96, 768), BF), ((48, 128), F32)],
        [
            buf(2, 4, 4), buf(2, 4, 4), buf(2, 2, 2), buf(2, 2, 2), buf(2, 2, 4),
            buf(2, 4), buf(2), buf(2), buf(2, 2),
            pltpu.VMEM((4, 96, 768), BF),
            pltpu.VMEM((96, 768), BF),
            pltpu.VMEM((96, 768), F32),
            pltpu.VMEM((96, 768), BF),
            pltpu.VMEM((48, 128), F32),
            pltpu.VMEM((4, 48, 128), F32),
            pltpu.VMEM((4, 48, 128), F32),
            pltpu.VMEM((4, 32, 128), F32),
            pltpu.VMEM((48, 128), F32),
            pltpu.VMEM((48, 128), F32),
            pltpu.VMEM((32, 128), F32),
        ],
        [g, n1, n2, x_rows, rows, v],
        [True, False, True, False, True, True],
        [True, False, True],
    )


def standardize(t):
    centered = t - jnp.mean(t, axis=-1, keepdims=True)
    rstd = lax.rsqrt(jnp.mean(centered * centered, axis=-1, keepdims=True) + norm_eps)
    return centered * rstd, rstd


def norm_back(u, xhat, rstd):
    return rstd * (
        u - jnp.mean(u, axis=-1, keepdims=True) - xhat * jnp.mean(u * xhat, axis=-1, keepdims=True)
    )


NN = (((1,), (0,)), ((), ()))
NT = (((1,), (1,)), ((), ()))
TN = (((0,), (0,)), ((), ()))
HEADS_HERE = (slice(0, 128), slice(128, 256), slice(256, 384))


def mm(a, b, dims):
    return lax.dot_general(a, b, dims, preferred_element_type=F32)


def low_half(shape):
    return lax.rem(lax.broadcasted_iota(jnp.int32, shape, 1), 128) < 64


def turn_head(t, tables_ref, sign):
    return (
        t * tables_ref[0]
        + sign * (pltpu.roll(t, 120, 1) * tables_ref[1] + pltpu.roll(t, 8, 1) * tables_ref[2])
    )


def pre_kernel(
    x_ref, g_ref, w_ref, bias_ref, upb_ref, tab_ref,
    n1_ref, n2_ref, gb_ref, a_ref, kv_ref, act_ref, gp_ref, gn_ref, rows_ref,
):
    vec = w_ref[:, 2304:2432].astype(F32).T
    xhat, _ = standardize(x_ref[...])
    n1_ref[...] = (xhat * vec[0:1] + vec[1:2]).astype(BF)
    n2_ref[...] = (xhat * vec[2:3] + vec[3:4]).astype(BF)
    grad = g_ref[...]
    gb_ref[...] = grad.astype(BF)
    qa = mm(n1_ref[...], w_ref[:, 1536:1920], NN) + bias_ref[0:1]
    ga = mm(gb_ref[...], w_ref[:, 1536:1920], NN)
    kv = mm(n1_ref[...], w_ref[:, 1920:2304], NN) + bias_ref[1:2]
    low = low_half((384, 128))
    for cols in HEADS_HERE:
        q = turn_head(qa[:, cols], tab_ref, 1.0).astype(BF).astype(F32) * 0.125
        a_ref[:, cols] = jnp.where(low, q, ga[:, cols]).astype(BF)
        kv_ref[:, cols] = turn_head(kv[:, cols], tab_ref, 1.0).astype(BF)
    pre = mm(n2_ref[...], w_ref[:, 0:768], NN) + upb_ref[...]
    cdf = 0.5 * (1.0 + lax.erf(pre * 0.7071067811865476))
    pdf = jnp.exp(-0.5 * pre * pre) * 0.3989422804014327
    act_ref[...] = (pre * cdf).astype(BF)
    gp = mm(gb_ref[...], w_ref[:, 768:1536], NN) * (cdf + pre * pdf)
    gp_ref[...] = gp.astype(BF)
    gn = mm(gp_ref[...], w_ref[:, 0:768], NT)
    gn_ref[...] = gn.astype(BF)
    rows_ref[0:1] = jnp.sum(gn * xhat, axis=0, keepdims=True)
    rows_ref[1:2] = jnp.sum(gn, axis=0, keepdims=True)
    rows_ref[2:3] = jnp.sum(grad, axis=0, keepdims=True) * 0.25
    rows_ref[3:4] = jnp.sum(gp, axis=0, keepdims=True)
    rows_ref[4:5] = vec[0:1]
    rows_ref[5:6] = vec[2:3]
    rows_ref[6:7] = vec[4:5] + vec[5:6]
    rows_ref[7:8] = jnp.zeros((1, 768), F32)


def spread_key_positions(pos_ref, kpos):
    x = lax.div(lax.axis_index("context"), 4)
    for m in range(4):
        kpos[384 * m : 384 * m + 384] = jnp.broadcast_to(pos_ref[x, m], (128, 384)).T


def allowed(kpos, pos_ref, j):
    kp = kpos[...]
    mine = lax.rem(lax.axis_index("context"), 4)
    return jnp.concatenate([kp, kp, kp], axis=1) <= pos_ref[j, mine]


def attention_forward_kernel(a_ref, kv_ref, pos_ref, o_ref, st_ref, kvt, kpos):
    spread_key_positions(pos_ref, kpos)
    low = low_half((384, 128))
    for h, cols in enumerate(HEADS_HERE):
        kvt[...] = kv_ref[:, cols].T

        def tile(j, _):
            a = a_ref[j, :, cols]
            aq = jnp.where(low, a, jnp.zeros_like(a))
            s = mm(kv_ref[:, cols], aq, NT)
            s = jnp.where(allowed(kpos, pos_ref, j), s, -1e30)
            top = jnp.max(s, axis=0, keepdims=True)
            p = jnp.exp(s - top)
            total = jnp.sum(p, axis=0, keepdims=True)
            o = mm(kvt[...], p.astype(BF), NN)[64:128]
            o = o / total
            gt = a.astype(F32).T[64:128]
            o_ref[j, 64 * h : 64 * h + 64, :] = o.astype(BF)
            st_ref[j, h : h + 1, :] = top + jnp.log(total)
            st_ref[j, 4 + h : 5 + h, :] = jnp.sum(o * gt, axis=0, keepdims=True)
            return 0

        lax.fori_loop(0, 4, tile, 0)
    st_ref[:, 3:4, :] = jnp.zeros((4, 1, 384), F32)
    st_ref[:, 7:8, :] = jnp.zeros((4, 1, 384), F32)


def attention_backward_kernel(
    a_ref, kv_ref, pos_ref, sts_ref, os_ref, act_ref, wd_ref, wa_ref,
    dq_ref, dkv_ref, att_ref, br_ref, kvt, kpos, acc_k, acc_v, st, wide_att,
):
    spread_key_positions(pos_ref, kpos)
    x = lax.div(lax.axis_index("context"), 4)
    parts = sts_ref[:, :, 0:4, :]
    top = jnp.max(parts, axis=0)
    norm = top + jnp.log(jnp.sum(jnp.exp(parts - top), axis=0))
    st[:, 0:4, :] = norm
    st[:, 4:8, :] = jnp.sum(jnp.exp(parts - norm) * sts_ref[:, :, 4:8, :], axis=0)
    share = jnp.exp(sts_ref[:, x, 0:4, :] - st[x, 0:4, :])
    for h in range(3):
        rows = slice(64 * h, 64 * h + 64)
        att = share[0, h : h + 1] * os_ref[0, rows].astype(F32)
        for i in (1, 2, 3):
            att = att + share[i, h : h + 1] * os_ref[i, rows].astype(F32)
        att_ref[rows] = att.astype(BF)
        wide_att[128 * h : 128 * h + 64] = jnp.zeros((64, 384), F32)
        wide_att[128 * h + 64 : 128 * h + 128] = att
    br_ref[...] = (
        mm(wide_att[...].T.astype(BF), wa_ref[...], NT) + mm(act_ref[...], wd_ref[...], NT)
    ).astype(BF)
    low = low_half((384, 128))
    for h, cols in enumerate(HEADS_HERE):
        kvt[...] = kv_ref[:, cols].T
        acc_k[...] = jnp.zeros_like(acc_k)
        acc_v[...] = jnp.zeros_like(acc_v)

        def tile(j, _):
            a = a_ref[j, :, cols]
            zero = jnp.zeros_like(a)
            kv = kv_ref[:, cols]
            s = mm(kv, jnp.where(low, a, zero), NT)
            p = jnp.where(allowed(kpos, pos_ref, j), jnp.exp(s - st[j, h : h + 1, :]), 0.0)
            gp = mm(kv, jnp.where(low, zero, a), NT)
            gs = (p * (gp - st[j, 4 + h : 5 + h, :])).astype(BF)
            acc_v[...] += mm(p.astype(BF), a, NN)
            acc_k[...] += mm(gs, a, NN)
            dq = mm(kvt[...], gs, NN)[0:64]
            dq_ref[j, 64 * h : 64 * h + 64, :] = (dq * 0.125).astype(BF)
            return 0

        lax.fori_loop(0, 4, tile, 0)
        dkv_ref[:, cols] = jnp.where(low_half((1536, 128)), acc_k[...], acc_v[...]).astype(BF)


def post_kernel(
    dq_ref, dkv_ref, att_ref, n1_ref, n2_ref, gb_ref, act_ref, gp_ref, w_ref, tab_ref, x_ref,
    rows_ref, g_ref, gn_ref, v_ref, wide, ga, gkv, big,
):
    dq = dq_ref[0].astype(F32)
    for i in (1, 2, 3):
        dq = dq + dq_ref[i].astype(F32)
    for h in range(3):
        wide[128 * h : 128 * h + 64] = dq[64 * h : 64 * h + 64]
        wide[128 * h + 64 : 128 * h + 128] = att_ref[64 * h : 64 * h + 64].astype(F32)
    packed = wide[...].T
    v_ref[...] = jnp.zeros_like(v_ref)
    for h, cols in enumerate(HEADS_HERE):
        t = turn_head(packed[:, cols], tab_ref, -1.0)
        v_ref[38 + h : 39 + h] = jnp.sum(t, axis=0, keepdims=True)
        ga[:, cols] = t.astype(BF)
        t = turn_head(dkv_ref[:, cols], tab_ref, -1.0)
        v_ref[41 + h : 42 + h] = jnp.sum(t, axis=0, keepdims=True)
        gkv[:, cols] = t.astype(BF)
    low = low_half((384, 384))
    t = ga[...]
    zero = jnp.zeros_like(t)
    only_q, only_att = jnp.where(low, t, zero), jnp.where(low, zero, t)
    gn = mm(only_q, w_ref[:, 0:384], NT) + mm(gkv[...], w_ref[:, 384:768], NT)
    gn_ref[...] = gn.astype(BF)
    xhat, _ = standardize(x_ref[...])
    sums = [
        jnp.sum(gn * xhat, axis=0, keepdims=True), jnp.sum(gn, axis=0, keepdims=True),
        rows_ref[0:1], rows_ref[1:2], rows_ref[2:3],
    ]
    for i, row in enumerate(sums):
        for j in range(6):
            v_ref[6 * i + j : 6 * i + j + 1] = row[:, 128 * j : 128 * j + 128]
    for j in range(6):
        v_ref[32 + j : 33 + j] = rows_ref[3:4, 128 * j : 128 * j + 128]
    for part in range(2):
        if part == 0:
            big[:, 0:768] = mm(n2_ref[...], gp_ref[...], TN)
            big[:, 768:1152] = mm(gb_ref[...], act_ref[:, 0:384], TN)
        else:
            big[:, 0:384] = mm(gb_ref[...], act_ref[:, 384:768], TN)
            big[:, 384:768] = mm(n1_ref[...], only_q, TN) + mm(gb_ref[...], only_att, TN)
            big[:, 768:1152] = mm(n1_ref[...], gkv[...], TN)
        for r in range(32):
            y, xx = (r // 2) % 2 * 2 + r // 16, (r // 4) % 4
            i, j = (xx, y) if part == 0 else (y, xx)
            g_ref[r % 2, part, i, j] = big[24 * r : 24 * r + 24].astype(BF)


def local_call(kernel, name, outs, scratch, args, specs=None):
    vspec = pl.BlockSpec(memory_space=pltpu.VMEM)
    specs = specs or {}

    def whole(shape):
        return pl.BlockSpec(shape, lambda i: (0,) * len(shape), pipeline_mode=pl.Buffered(1))

    return pl.pallas_call(
        kernel,
        name=name,
        grid=(1,),
        out_shape=[jax.ShapeDtypeStruct(*o) for o in outs],
        in_specs=[specs.get(n) or whole(a.shape) for n, a in enumerate(args)],
        out_specs=[whole(o[0]) for o in outs],
        scratch_shapes=scratch,
        compiler_params=pltpu.CompilerParams(vmem_limit_bytes=60 * 1024 * 1024),
    )(*args)


def columns(width, block):
    return pl.BlockSpec((768, width), lambda i: (0, block), pipeline_mode=pl.Buffered(1))


def shards(
    layer_input_residual, positions, ln1_gain, ln1_bias, ln2_gain, ln2_bias, w_qkv,
    query_key_value_bias, w_out, b_out, w_up, up_bias_vector, w_down, b_down, grad_out,
):
    c = lax.axis_index("context")
    x_in = layer_input_residual[0]
    g_in = grad_out[0]

    def pair(a, b):
        n = a.shape[0]
        both = jnp.stack([a.reshape(n, 3, HS), b.reshape(n, 3, HS)], axis=2)
        return both.reshape(n, 384)

    vec = jnp.stack([ln1_gain, ln1_bias, ln2_gain, ln2_bias, b_out, b_down], axis=1)
    src = jnp.concatenate(
        [
            w_up, w_down, pair(w_qkv[:, 0], w_out), pair(w_qkv[:, 1], w_qkv[:, 2]),
            jnp.pad(vec, ((0, 0), (0, 122))),
        ],
        axis=1,
    )
    whole = gather_weights(src).reshape(768, WCOLS)
    qb = query_key_value_bias
    bias = jnp.concatenate(
        [pair(qb[0:1], jnp.zeros_like(qb[0:1])), pair(qb[1:2], qb[2:3])], axis=0
    )
    own_pos = lax.dynamic_slice_in_dim(positions.reshape(16, 384), c, 1, 0)[0]
    lane = jnp.arange(128)
    freqs = jnp.exp(-(lax.rem(lane, 8).astype(F32) * (2.0 / ROT)) * math.log(10000.0))
    angles = own_pos.astype(F32)[:, None] * freqs
    sine = jnp.sin(angles)
    tables = jnp.stack(
        [
            jnp.where(lane < 16, jnp.cos(angles), 1.0),
            jnp.where(lane < 8, -sine, 0.0),
            jnp.where((lane >= 8) & (lane < 16), sine, 0.0),
        ]
    )
    pos_f = positions.astype(F32).reshape(4, 4, 1, 384)

    tok, sq = ((384, 768), BF), ((384, 384), BF)
    n1, n2, gb, a_own, kv_own, act, gp, g_n2, rows = local_call(
        pre_kernel, "pre",
        [tok, tok, tok, sq, sq, tok, tok, tok, ((8, 768), F32)], [],
        [x_in, g_in, whole, bias, up_bias_vector.reshape(1, 768), tables],
    )
    a_all, kv_all, n2_parts = gather_attention(a_own, kv_own, g_n2.reshape(4, 96, 768))
    kv_flat = kv_all.reshape(1536, 384)
    keys_t = [pltpu.VMEM((128, 1536), BF), pltpu.VMEM((1536, 128), F32)]
    o_part, st_part = local_call(
        attention_forward_kernel, "attention_forward",
        [((4, 192, 384), BF), ((4, 8, 384), F32)], keys_t, [a_all, kv_flat, pos_f],
    )
    o_all, st_all = share_partials(o_part, st_part)
    acc = pltpu.VMEM((1536, 128), F32)
    dq_part, dkv_part, attended, branch = local_call(
        attention_backward_kernel, "attention_backward",
        [((4, 192, 384), BF), ((1536, 384), BF), ((192, 384), BF), tok],
        keys_t + [acc, acc, pltpu.VMEM((4, 8, 384), F32), pltpu.VMEM((384, 384), F32)],
        [a_all, kv_flat, pos_f, st_all, o_all, act, whole, whole],
        {6: columns(768, 1), 7: columns(384, 4)},
    )
    dq_all, dkv, br_all = reduce_attention(
        dq_part, dkv_part.reshape(4, 384, 384), branch.reshape(4, 96, 768)
    )
    layer_out = x_in + br_all.reshape(384, 768).astype(F32) + rows[6]
    grads, g_n1, small = local_call(
        post_kernel, "post",
        [((2, 2, 4, 4, 24, GHALF), BF), tok, ((48, 128), F32)],
        [
            pltpu.VMEM((384, 384), F32), pltpu.VMEM((384, 384), BF),
            pltpu.VMEM((384, 384), BF), pltpu.VMEM((768, GHALF), F32),
        ],
        [dq_all, dkv, attended, n1, n2, gb, act, gp, whole, tables, x_in, rows],
        {8: columns(768, 2)},
    )
    own_w, pieces, small = reduce_weights(
        grads, g_n1.reshape(4, 96, 768), n2_parts, x_in.reshape(4, 96, 768), rows, small
    )
    grad_in = g_in + pieces.reshape(384, 768).astype(F32)
    mine = lax.axis_index("shard") * 16 + c
    own_vec = lax.dynamic_slice_in_dim(small[:30].reshape(5, 768), mine * 24, 24, 1)
    own_a = own_w[:, 1536:1920].reshape(24, 3, 2, HS)
    own_kv = own_w[:, 1920:2304].reshape(24, 3, 2, HS)
    own_qkv = jnp.stack(
        [t.reshape(24, 192) for t in (own_a[:, :, 0], own_kv[:, :, 0], own_kv[:, :, 1])], axis=1
    )
    b_a, b_kv = small[38:41].reshape(3, 2, HS), small[41:44].reshape(3, 2, HS)
    g_b_qkv = jnp.stack([t.reshape(192) for t in (b_a[:, 0], b_kv[:, 0], b_kv[:, 1])])
    return (
        layer_out[None], grad_in[None],
        own_vec[0], own_vec[1], own_vec[2], own_vec[3],
        own_qkv, g_b_qkv,
        own_a[:, :, 1].reshape(24, 192),
        own_vec[4],
        own_w[:, :768],
        small[32:38].reshape(768),
        own_w[:, 768:1536],
        own_vec[4],
    )


def solution(mesh):
    rows = P(("shard", "context"))
    token = P("shard", "context", None)
    wide = P(("shard", "context"), "tensor")
    qkv = P(("shard", "context"), None, "tensor")
    in_specs = (
        token, P("shard", None), rows, rows, rows, rows, qkv, P(None, "tensor"),
        wide, rows, wide, P("tensor"), wide, rows, token,
    )
    out_specs = (
        token, token, rows, rows, rows, rows, qkv, P(None, "tensor"),
        wide, rows, wide, P("tensor"), wide, rows,
    )
    return jax.shard_map(shards, mesh=mesh, in_specs=in_specs, out_specs=out_specs, check_vma=False)
```

time: 261 us -> 189 us (0.72)
  local copies, waits for them, and re-layouts: 39.7 us -> 13.5 us
  matrix products: 23.5 us -> 0 us
  other arithmetic: 24.8 us -> 7.96 us
  Pallas kernels: 171 us -> 166 us
    dot_general x12 -> x0, matrix products: 23.5 us -> none  [dot(): return jnp.einsum(spec, a, b, preferred_element_type=F32)]
    pallas_call x6 -> x5, Pallas kernels: 127 us -> 104 us  [comm_call(): pl.pallas_call(kernel, name=name, out_shape=[jax.ShapeDtypeStruct(*o) for...]
    pallas_call x2 -> x4, Pallas kernels: 44.2 us -> 62.4 us  [local_call(): pl.pallas_call(kernel, name=name, grid=(1,), out_shape=[jax.ShapeDtypeStr...]
    reduce_sum x11 -> x0, other arithmetic: 10.6 us -> none  [the longest x1 2.01 us: shards(): jnp.sum(s2, axis=0)]
    reshape x9 -> x10, local copies, waits for them, and re-layouts: 10.2 us -> 2.58 us  [the longest x1 1.27 us: shards(): small[32:38].reshape(768)]
    slice x13 -> x10, local copies, waits for them, and re-layouts: 11.9 us -> 4.96 us  [the longest x1 1.58 us: shards(): own_w[:, 768:1536]]
    concatenate x2 -> x1, local copies, waits for them, and re-layouts: 4.67 us -> 0.01 us  [shards(): jnp.concatenate([w_up, w_down, pair(w_qkv[:, 0], w_out), pair(w_qkv[:, 1]...]
    transpose x2 -> x0, local copies, waits for them, and re-layouts: 2.67 us -> none  [the longest x1 2.41 us: shards(): grads[..., 0, :].transpose(3, 1, 2, 0, 4, 5).reshape(2, 4, 4, 24, GHALF)]
where the time goes in v2:
time: 189 us
  Pallas kernels  166 us (88%)
  local copies, waits for them, and re-layouts  13.5 us (7%)
  other arithmetic  7.96 us (4%)
    pallas_call x5, Pallas kernels, comm_call(): pl.pallas_call(kernel, name=name, out_shape=[jax.ShapeDtypeStruct(*o) for...  104 us
    pallas_call x4, Pallas kernels, local_call(): pl.pallas_call(kernel, name=name, grid=(1,), out_shape=[jax.ShapeDtypeStr...  62.4 us

profile of v2, /device:TPU:1, one launch (start us, length us, event | category | flops | bytes accessed | tf_op | source)
XLA Modules:
  0.0 188.8 jit_solution(1968640948256412940)
XLA Ops:
  0.7 0.5 broadcast.247
  1.2 2.1 %fusion.9 = (f32[1,6144]{1,0:T(1,128)}, s32[6144]{0:T(1024)S(1)}) fusion(s32[1,6144]{1,0:T(1,128)} %param.16, s32[]{:T(128)} %broadcast.247), kind=kLoop, calls=%fused_computation.48 | loop fusion | flops 6144 | bytes 73732 | tf_op jit(solution)/shard_map/convert_element_type | solution.py:838
  3.4 0.8 fusion.4
  4.2 0.9 pad_maximum_fusion.tab_ref
  5.1 0.1 stack_reshape_squeeze.28
  5.4 0.1 reshape.334
  5.7 0.1 reshape.333
  6.0 0.1 copy.54
  6.1 0.6 copy-done.4
  6.7 24.6 %gather_weights.1 = bf16[32,24,2432]{2,1,0:T(8,128)(2,1)} custom-call(bf16[24,2432]{1,0:T(8,128)(2,1)} %copy-done.4), custom_call_target="tpu_custom_call" | custom-call | tf_op jit(solution)/shard_map/gather_weights/pallas_call | solution.py:90
  31.4 0.1 stack_reshape.15
  31.5 0.1 stack_reshape.16
  31.6 0.1 reshape.337
  31.7 0.1 reshape.336
  31.8 0.6 pad_maximum_fusion.6.bias_ref
  32.4 0.6 reshape.338.upb_ref
  33.0 6.6 %pre.1 = (bf16[384,768]{1,0:T(8,128)(2,1)}, bf16[384,768]{1,0:T(8,128)(2,1)}, bf16[384,768]{1,0:T(8,128)(2,1)}, bf16[384,384]{1,0:T(8,128)(2,1)}, bf16[384,384]{...) custom-call(f32[384,768]{1,0:T(8,128)} %bitcast.46, ...), custom_call_target="tpu_custom_call" | custom-call | tf_op jit(solution)/shard_map/pre/pallas_call | solution.py:784
  39.6 17.3 %gather_attention.1 = (bf16[4,384,384]{2,1,0:T(8,128)(2,1)}, bf16[4,384,384]{2,1,0:T(8,128)(2,1)}, bf16[4,96,768]{2,1,0:T(8,128)(2,1)}) custom-call(bf16[384,384]{1,0:T(8,128)(2,1)} %get-tuple-element.43.a_ref, bf16[384,384]{1,0:T(8,128)(2,1)} %get-tuple-element.44.kv_ref, bf16[4,96,768]{2,1,0:T(8,128)(2,1)} %bitcast.54), custom_call_target="tpu_custom_call" | custom-call | tf_op jit(solution)/shard_map/gather_attention/pallas_call | solution.py:90
  56.9 18.4 %attention_forward.1 = (bf16[4,192,384]{2,1,0:T(8,128)(2,1)}, f32[4,8,384]{2,1,0:T(8,128)}) custom-call(bf16[4,384,384]{2,1,0:T(8,128)(2,1)} %get-tuple-element.46.a_ref, bf16[1536,384]{1,0:T(8,128)(2,1)} %bitcast.49, f32[4,4,1,384]{3,2,1,0:T(1,128)} %bitcast.58), custom_call_target="tpu_custom_call" | custom-call | tf_op jit(solution)/shard_map/attention_forward/pallas_call | solution.py:784
  75.3 12.4 %share_partials.1 = (bf16[4,192,384]{2,1,0:T(8,128)(2,1)}, f32[4,4,8,384]{3,2,1,0:T(8,128)}) custom-call(bf16[4,192,384]{2,1,0:T(8,128)(2,1)} %get-tuple-element.48.o_ref, f32[4,8,384]{2,1,0:T(8,128)} %get-tuple-element.49.st_ref), custom_call_target="tpu_custom_call" | custom-call | tf_op jit(solution)/shard_map/share_partials/pallas_call | solution.py:90
  87.7 28.5 %attention_backward.1 = (bf16[4,192,384]{2,1,0:T(8,128)(2,1)}, bf16[1536,384]{1,0:T(8,128)(2,1)}, bf16[192,384]{1,0:T(8,128)(2,1)}, bf16[384,768]{1,0:T(8,128)(2,1)}) custom-call(bf16[4,384,384]{2,1,0:T(8,128)(2,1)} %get-tuple-element.46.a_ref, bf16[1536,384]{1,0:T(8,128)(2,1)} %bitcast.50, f32[4,4,1,384]{3,2,1,0:T(1,128)} %bitcast.59, ...), custom_call_target="tpu_custom_call" | custom-call | tf_op jit(solution)/shard_map/attention_backward/pallas_call | solution.py:784
  116.2 18.2 %reduce_attention.1 = (bf16[4,192,384]{2,1,0:T(8,128)(2,1)}, f32[384,384]{1,0:T(8,128)}, bf16[4,96,768]{2,1,0:T(8,128)(2,1)}) custom-call(bf16[4,192,384]{2,1,0:T(8,128)(2,1)} %get-tuple-element.53.dq_ref, bf16[4,384,384]{2,1,0:T(8,128)(2,1)} %bitcast.52, bf16[4,96,768]{2,1,0:T(8,128)(2,1)} %bitcast.57), custom_call_target="tpu_custom_call" | custom-call | tf_op jit(solution)/shard_map/reduce_attention/pallas_call | solution.py:90
  134.4 8.9 %post.1 = (bf16[2,2,4,4,24,1152]{5,4,3,2,1,0:T(8,128)(2,1)}, bf16[384,768]{1,0:T(8,128)(2,1)}, f32[48,128]{1,0:T(8,128)}) custom-call(bf16[4,192,384]{2,1,0:T(8,128)(2,1)} %get-tuple-element.58.dq_ref, f32[384,384]{1,0:T(8,128)} %get-tuple-element.59.dkv_ref, bf16[192,384]{1,0:T(8,128)(2,1)} %get-tuple-element.60.att_ref, ...), custom_call_target="tpu_custom_call" | custom-call | tf_op jit(solution)/shard_map/post/pallas_call | solution.py:784
  143.3 31.5 %reduce_weights.1 = (f32[24,2304]{1,0:T(8,128)}, bf16[4,96,768]{2,1,0:T(8,128)(2,1)}, f32[48,128]{1,0:T(8,128)}) custom-call(bf16[2,2,4,4,24,1152]{5,4,3,2,1,0:T(8,128)(2,1)} %get-tuple-element.65.g_ref, bf16[4,96,768]{2,1,0:T(8,128)(2,1)} %bitcast.53, bf16[4,96,768]{2,1,0:T(8,128)(2,1)} %get-tuple-element.67.n2_ref, f32[4,96,768]{2,1,0:T(8,128)} %bitcast.48, ...), custom_call_target="tpu_custom_call" | custom-call | tf_op jit(solution)/shard_map/reduce_weights/pallas_call | solution.py:90
  174.8 0.8 fusion.8
  175.6 0.1 reshape.350
  175.7 0.1 stack_reshape_squeeze.34
  175.9 0.1 reshape.349
  176.0 0.1 stack_reshape_squeeze.33
  176.1 0.6 pad_maximum_fusion.5
  176.7 0.8 fusion.6
  177.5 0.1 reshape.347
  177.6 0.8 slice_reduce_fusion
  178.3 0.1 stack_reshape_squeeze.30
  178.4 0.1 reshape.348
  178.6 0.2 slice_reduce_fusion.2
  178.8 0.1 stack_reshape_squeeze.31
  178.9 0.1 stack_reshape_squeeze.32
  179.0 0.6 pad_maximum_fusion.1
  179.6 1.1 convert_add_fusion
  180.7 1.5 reshape_squeeze.7
  182.2 1.6 fusion.5
  183.8 0.7 slice.89
  184.6 0.5 slice_bitcast_fusion.1
  185.2 1.3 slice_bitcast_fusion
  186.4 0.8 slice_reduce_fusion.4
  187.2 1.1 fusion
  188.3 0.5 copy.63
  (64 shorter events, 1.0 us)
Async XLA Ops:
  0.6 4.4 %copy-start.5 = (bf16[24,3,192]{2,0,1:T(8,128)(2,1)S(1)}, bf16[24,3,192]{2,0,1:T(8,128)(2,1)}, u32[]{:S(2)}) copy-start(bf16[24,3,192]{2,0,1:T(8,128)(2,1)} %param.21) | copy-start | bytes 82948
  0.7 4.9 %copy-start.8 = (bf16[24,192]{1,0:T(8,128)(2,1)S(1)}, bf16[24,192]{1,0:T(8,128)(2,1)}, u32[]{:S(2)}) copy-start(bf16[24,192]{1,0:T(8,128)(2,1)} %param.23) | copy-start | bytes 27652
  3.3 2.5 %copy-start.6 = (bf16[24,768]{1,0:T(8,128)(2,1)S(1)}, bf16[24,768]{1,0:T(8,128)(2,1)}, u32[]{:S(2)}) copy-start(bf16[24,768]{1,0:T(8,128)(2,1)} %param.25) | copy-start | bytes 110596
  3.4 2.5 %copy-start.7 = (bf16[24,768]{1,0:T(8,128)(2,1)S(1)}, bf16[24,768]{1,0:T(8,128)(2,1)}, u32[]{:S(2)}) copy-start(bf16[24,768]{1,0:T(8,128)(2,1)} %param.27) | copy-start | bytes 110596
  4.2 1.7 copy-start.11
  4.2 1.7 copy-start.12
  4.2 1.7 copy-start.13
  4.2 1.7 copy-start.14
  4.2 1.7 copy-start.15
  4.2 1.7 copy-start.16
  6.1 0.6 copy-start.4
  6.7 24.6 %copy-start.10 = (f32[3,192]{1,0:T(4,128)S(1)}, f32[3,192]{1,0:T(4,128)}, u32[]{:S(2)}) copy-start(f32[3,192]{1,0:T(4,128)} %param.22) | copy-start | bytes 6916
  6.7 25.7 %copy-start.9 = (f32[768]{0:T(1024)S(1)}, f32[768]{0:T(1024)}, u32[]{:S(2)}) copy-start(f32[768]{0:T(1024)} %param.26) | copy-start | bytes 9220
  143.3 36.3 %copy-start.1 = (f32[1,384,768]{2,1,0:T(8,128)S(1)}, f32[1,384,768]{2,1,0:T(8,128)}, u32[]{:S(2)}) copy-start(f32[1,384,768]{2,1,0:T(8,128)} %param.29) | copy-start | bytes 3538948
  174.8 4.8 %copy-start.3 = (bf16[4,96,768]{2,1,0:T(8,128)(2,1)S(1)}, bf16[4,96,768]{2,1,0:T(8,128)(2,1)}, u32[]{:S(2)}) copy-start(bf16[4,96,768]{2,1,0:T(8,128)(2,1)} %get-tuple-element.69) | copy-start | bytes 1769476
  179.6 7.6 %copy-start = (f32[1,384,768]{2,1,0:T(8,128)S(1)}, f32[1,384,768]{2,1,0:T(8,128)}, u32[]{:S(2)}) copy-start(f32[1,384,768]{2,1,0:T(8,128)} %param.15) | copy-start | bytes 3538948
  179.6 7.6 %copy-start.2 = (bf16[4,96,768]{2,1,0:T(8,128)(2,1)S(1)}, bf16[4,96,768]{2,1,0:T(8,128)(2,1)}, u32[]{:S(2)}) copy-start(bf16[4,96,768]{2,1,0:T(8,128)(2,1)} %get-tuple-element.56) | copy-start | bytes 1769476
  185.2 3.2 %copy-start.17 = (f32[24]{0:T(128)}, f32[24]{0:T(128)S(1)}, u32[]{:S(2)}) copy-start(f32[24]{0:T(128)S(1)} %get-tuple-element.129) | copy-start | bytes 292
